TPU v7x, 512 devices: a whole 4x4x16 slice. The times are simulated.
512 devices in a mesh: cls: 16 (over x, y), pose: 32 (over z, core).
Axes of the slice: x: 4, y: 4, z: 16, core: 2. Of those that a mesh axis runs over, the one named last changes fastest.
Arguments:
- images: bfloat16 [512, 16384], P(('pose', 'cls')), may hold values from -6 to 6
- significant: int32 [512, 3], P(('pose', 'cls')), may hold values from 0 to 31, all different within a row; in each aligned block of 16 rows (0 to 15, 16 to 31, ...) at most 3 rows name the same one
- projections: bfloat16 [32, 512, 16384], P('cls', 'pose')
- phase: float32 [4, 8192], replicated, may hold values from -3.140625 to 3.140625
Outputs:
- back_sums: bfloat16 [32, 512, 16384], P('cls', 'pose')
- evidence: float32 [512], P(('pose', 'cls'))
Inputs may be any that keep to these rules, and one draw needn't show every extreme that they name: `significant`: each particle names 3 different bins. Of the particles of one aligned block of 16 rows, at most 3 name one bin.
All inputs are finite; a program needn't handle non-finite values.
Results may differ from a plain program's by a relative error of at most 0.012.
The roundings to bfloat16 on the way count: a program that leaves them out, or rounds other values in their place, can miss the bound.
Values may be sent and summed in bfloat16 or wider, within the bound.
No kernel may reach another device: no remote copies, remote signals or barrier semaphores. Data moves between devices by JAX's collectives and lax.ppermute only.
A program may use at most 64 MiB of HBM per device.

v0:
```python
import jax
import jax.numpy as jnp
from jax import lax
from jax.sharding import PartitionSpec as P


def rotate(block, cosv, sinv, coef):
    real = block[:, :coef]
    imag = block[:, coef:]
    return jnp.concatenate([cosv * real - sinv * imag, sinv * real + cosv * imag], axis=1)


def unrotate(block, cosv, sinv, coef):
    real = block[:, :coef]
    imag = block[:, coef:]
    return jnp.concatenate([cosv * real + sinv * imag, cosv * imag - sinv * real], axis=1)


def per_device(images, significant, projections, phase):
    gathered, gathered_bins = (
        lax.all_gather(images, "cls", axis=0, tiled=True),
        lax.all_gather(significant, "cls", axis=0, tiled=True),
    )
    group_rows, per_row = gathered_bins.shape
    bin_count = lax.axis_size("pose")
    capacity = 2 * group_rows * per_row // bin_count
    flat_bins = gathered_bins.reshape(-1)
    owner_row = jnp.arange(group_rows * per_row, dtype=jnp.int32) // per_row
    one_hot = (flat_bins[:, None] == jnp.arange(bin_count, dtype=jnp.int32)[None, :]).astype(
        jnp.int32
    )
    before = jnp.cumsum(one_hot, axis=0) - one_hot
    position = jnp.sum(before * one_hot, axis=1)
    slot = flat_bins * capacity + position
    source = jnp.full((bin_count * capacity,), group_rows, jnp.int32).at[slot].set(owner_row)
    width = gathered.shape[1]
    coef = width // 2
    outgoing = jnp.take(gathered, source, axis=0, mode="fill", fill_value=0).reshape(
        bin_count, capacity, width
    )
    local_classes, pose_count, _ = projections.shape
    pair_count = local_classes * pose_count
    flat_proj = projections.reshape(pair_count, width).astype(jnp.float32)
    cosv = jnp.cos(phase)
    sinv = jnp.sin(phase)
    shift_count = phase.shape[0]
    shifted = [
        rotate(flat_proj, cosv[step], sinv[step], coef).astype(jnp.bfloat16)
        for step in range(shift_count)
    ]
    incoming = lax.all_to_all(outgoing, "pose", split_axis=0, concat_axis=0, tiled=True)
    rows = incoming.reshape(-1, width)
    parts = [
        lax.dot_general(rows, table, (((1,), (1,)), ((), ())), preferred_element_type=jnp.float32)
        for table in shifted
    ]
    scores = jnp.stack(parts, axis=1).reshape(
        incoming.shape[0], incoming.shape[1], shift_count, pair_count
    )
    slot_top = jnp.max(scores, axis=(2, 3))
    slot_total = jnp.sum(jnp.exp(scores - slot_top[:, :, None, None]), axis=(2, 3))
    home_top, home_total = (
        lax.all_to_all(slot_top, "pose", split_axis=0, concat_axis=0, tiled=True),
        lax.all_to_all(slot_total, "pose", split_axis=0, concat_axis=0, tiled=True),
    )
    tops = jnp.take(home_top.reshape(-1), slot).reshape(group_rows, per_row)
    totals = jnp.take(home_total.reshape(-1), slot).reshape(group_rows, per_row)
    group_top = jnp.max(tops, axis=1)
    group_total = jnp.sum(totals * jnp.exp(tops - group_top[:, None]), axis=1)
    overall_top = lax.pmax(group_top, "cls")
    overall_total = lax.psum(group_total * jnp.exp(group_top - overall_top), "cls")
    evidence_all = overall_top + jnp.log(overall_total)
    own_rows = images.shape[0]
    own_evidence = lax.dynamic_slice_in_dim(
        evidence_all, lax.axis_index("cls") * own_rows, own_rows
    )
    slot_evidence = jnp.take(evidence_all, source, mode="fill", fill_value=0.0).reshape(
        bin_count, capacity
    )
    incoming_evidence = lax.all_to_all(
        slot_evidence, "pose", split_axis=0, concat_axis=0, tiled=True
    )
    rows = incoming.reshape(-1, width)
    level = incoming_evidence.reshape(-1)
    accum = jnp.zeros((pair_count, width), jnp.float32)
    for step in range(shift_count):
        step_scores = scores[:, :, step, :].reshape(-1, pair_count)
        weight = jnp.exp(step_scores - level[:, None]).astype(jnp.bfloat16)
        partial_sum = lax.dot_general(
            weight, rows, (((0,), (0,)), ((), ())), preferred_element_type=jnp.float32
        )
        accum = accum + unrotate(partial_sum, cosv[step], sinv[step], coef)
    back_sums = accum.astype(jnp.bfloat16).reshape(projections.shape)
    return (back_sums, own_evidence)


def solution(mesh):
    placed = (P(("pose", "cls"), None), P(("pose", "cls"), None), P("cls", "pose", None), P())
    return jax.shard_map(
        per_device,
        mesh=mesh,
        in_specs=placed,
        out_specs=(P("cls", "pose", None), P(("pose", "cls"))),
        check_vma=False,
    )
```

profile of v0, /device:TPU:1, one launch (start us, length us, event | category | flops | bytes accessed | tf_op | source)
XLA Modules:
  0.0 440.7 jit_solution(492076923430727885)
XLA Ops:
  0.6 17.3 %all-gather = s32[16,1,3]{2,1,0:T(1,128)S(1)} all-gather(s32[1,1,3]{2,1,0:T(1,128)} %bitcast.87), channel_id=1, replica_groups=mesh['cls'=16,'pose'=32] {'cls'}, dimensions={0}, use_global_device_ids=true | all-gather | bytes 204 | tf_op jit(solution)/shard_map/all_gather | solution.py:22
  18.0 0.5 broadcast.163
  18.5 0.7 fusion.38
  19.5 0.2 select_reduce_fusion
  19.7 0.7 scatter_custom_fusion
  20.5 18.3 %all-gather.1 = bf16[16,1,16384]{2,1,0:T(2,128)(2,1)S(1)} all-gather(bf16[1,1,16384]{2,1,0:T(2,128)(2,1)} %bitcast.84), channel_id=1, replica_groups=mesh['cls'=16,'pose'=32] {'cls'}, dimensions={0}, use_global_device_ids=true | all-gather | bytes 557056 | tf_op jit(solution)/shard_map/all_gather | solution.py:21
  38.8 0.6 copy.32
  39.4 4.2 gather_fusion
  43.6 5.2 %gather.14 = bf16[32,3,16384]{2,1,0:T(4,128)(2,1)} reshape(bf16[96,16384]{1,0:T(8,128)(2,1)} %gather_fusion) | data formatting | bytes 6291456 | tf_op jit(solution)/shard_map/jit(_take)/gather | solution.py:38
  48.8 0.1 broadcast_in_dim.34
  48.9 5.9 %broadcast_select_fusion = bf16[32,3,16384]{2,1,0:T(4,128)(2,1)} fusion(bf16[32,3,16384]{2,1,0:T(4,128)(2,1)} %gather.14, pred[32,3]{1,0:T(8,128)(4,1)S(1)} %broadcast_in_dim.34), kind=kLoop, calls=%fused_computation.4 | loop fusion | flops 1572864 | bytes 6291552 | tf_op jit(solution)/shard_map/jit(_take)/select_n | solution.py:38
  54.9 25.8 %all-to-all-start = ((bf16[32,3,16384]{2,1,0:T(4,128)(2,1)}), bf16[32,3,16384]{2,1,0:T(4,128)(2,1)}, u32[]{:S(2)}, u32[]{:S(2)}) async-start(bf16[32,3,16384]{2,1,0:T(4,128)(2,1)} %broadcast_select_fusion), calls=%async_computation | async-start | bytes 8388608 | tf_op jit(solution)/shard_map/all_to_all | solution.py:51
  80.6 1.0 fusion.41
  81.6 0.2 fusion.39
  81.8 0.2 bitcast_convert_fusion
  82.0 1.3 subtract_convert_fusion.3
  83.3 2.2 subtract_convert_fusion.2
  85.5 178.5 %all-to-all-done = bf16[32,3,16384]{2,1,0:T(4,128)(2,1)} async-done(((bf16[32,3,16384]{2,1,0:T(4,128)(2,1)}), bf16[32,3,16384]{2,1,0:T(4,128)(2,1)}, u32[]{:S(2)}, u32[]{:S(2)}) %all-to-all-start) | async-done | bytes 3145760 | tf_op jit(solution)/shard_map/all_to_all | solution.py:51
  264.0 4.6 %reshape.223 = bf16[96,16384]{1,0:T(8,128)(2,1)S(1)} reshape(bf16[32,3,16384]{2,1,0:T(4,128)(2,1)} %all-to-all-done) | data formatting | bytes 6291456 | tf_op jit(solution)/shard_map/reshape | solution.py:52
  268.5 3.0 fusion.43
  271.5 0.6 copy-done.2
  272.2 3.0 fusion.44
  275.3 0.6 copy-done.4
  275.8 0.7 copy.23
  276.6 0.8 stack.17
  277.4 3.6 fusion.46
  280.9 1.4 copy.22
  282.4 1.4 stack.16
  283.8 3.5 fusion.45
  287.3 1.4 copy.21
  288.8 1.4 stack.15
  290.2 0.7 maximum_maximum_fusion
  290.9 0.7 reduce_max.76
  291.6 1.7 fusion.20
  293.3 10.3 %all-to-all-start.2 = ((f32[32,1,3]{2,1,0:T(1,128)}), f32[32,1,3]{2,1,0:T(1,128)S(1)}, u32[]{:S(2)}, u32[]{:S(2)}) async-start(f32[32,1,3]{2,1,0:T(1,128)} %bitcast.85), calls=%async_computation.2 | async-start | bytes 32768 | tf_op jit(solution)/shard_map/all_to_all | solution.py:64
  303.6 0.7 reduce_max.74
  304.4 11.1 %all-to-all-done.2 = f32[32,1,3]{2,1,0:T(1,128)S(1)} async-done(((f32[32,1,3]{2,1,0:T(1,128)}), f32[32,1,3]{2,1,0:T(1,128)S(1)}, u32[]{:S(2)}, u32[]{:S(2)}) %all-to-all-start.2) | async-done | bytes 416 | tf_op jit(solution)/shard_map/all_to_all | solution.py:64
  315.4 4.4 all-to-all-start.1
  319.8 0.6 broadcast.164
  320.4 0.7 reduce.26
  321.3 10.4 %all-to-all-done.1 = f32[32,1,3]{2,1,0:T(1,128)S(1)} async-done(((f32[32,1,3]{2,1,0:T(1,128)}), f32[32,1,3]{2,1,0:T(1,128)S(1)}, u32[]{:S(2)}, u32[]{:S(2)}) %all-to-all-start.1) | async-done | bytes 416 | tf_op jit(solution)/shard_map/all_to_all | solution.py:63
  331.7 0.7 reduce.25
  332.4 0.1 reshape.224
  332.5 0.8 gather_fusion.2
  333.3 0.8 gather_fusion.1
  334.2 0.1 reduce_max.75
  334.3 30.9 %pmax.7 = f32[16]{0:T(128)S(1)} all-reduce(f32[16]{0:T(128)S(1)} %reduce_max.75), channel_id=1, replica_groups=mesh['cls'=16,'pose'=32] {'cls'}, use_global_device_ids=true, to_apply=%region_8.10 | all-reduce | flops 16 | bytes 128 | tf_op jit(solution)/shard_map/pmax | solution.py:70
  365.2 0.2 multiply_reduce_fusion.1
  365.5 28.5 %psum.7 = f32[16]{0:T(128)S(1)} all-reduce(f32[16]{0:T(128)S(1)} %exponential_multiply_fusion), channel_id=1, replica_groups=mesh['cls'=16,'pose'=32] {'cls'}, use_global_device_ids=true, to_apply=%region_11.13 | all-reduce | flops 16 | bytes 128 | tf_op jit(solution)/shard_map/psum | solution.py:71
  394.0 0.7 fusion.42
  394.7 9.8 %fusion.30 = f32[96]{0:T(128)S(1)} fusion(f32[]{:T(128)} %bitcast.16, f32[]{:T(128)} %bitcast.17, f32[]{:T(128)} %bitcast.18, f32[]{:T(128)} %bitcast.19, f32[]{:T(128)} %bitcast.20, f32[]{:T(128)} %bitcast.21, f32[]{:T(128)} %bitcast.22, f32[]{:T(128)} %bitcast.23, f32[]{:T(128)} %bitcast.24, f32[]{:T(128)} %bitcast.25, f32[]{:T(128)} %bitcast.26, ...), kind=kLoop, calls=%fused_computation.89 | loop fusion | flops 3552 | bytes 832 | tf_op jit(solution)/shard_map/jit(_take)/select_n | solution.py:77
  404.6 29.6 %all_to_all.26 = f32[32,1,3]{2,1,0:T(1,128)S(1)} all-to-all(f32[32,1,3]{2,1,0:T(1,128)S(1)} %bitcast.86), channel_id=1, replica_groups=mesh['cls'=16,'pose'=32] {'pose'}, dimensions={0} | all-to-all | bytes 768 | tf_op jit(solution)/shard_map/all_to_all | solution.py:80
  434.2 0.7 reduce.27
  435.0 1.3 fusion.22
  436.3 0.6 fusion.23
  436.9 0.1 copy-done.5
  437.1 0.6 fusion.24
  437.6 0.2 copy-done.3
  437.8 0.6 fusion.25
  438.3 0.3 multiply_add_fusion.3
  438.6 0.2 multiply_add_fusion.2
  438.9 0.2 multiply_add_fusion.1
  439.1 0.2 multiply_add_fusion
  439.4 1.3 fusion.2
  (31 shorter events, 1.0 us)
Async XLA Ops:
  54.8 25.8 %copy-start.1 = (f32[4,8192]{1,0:T(4,128)S(1)}, f32[4,8192]{1,0:T(4,128)}, u32[]{:S(2)}) copy-start(f32[4,8192]{1,0:T(4,128)} %param.9) | copy-start | bytes 393220
  54.8 26.9 %copy-start = (bf16[2,16,16384]{2,1,0:T(8,128)(2,1)S(1)}, bf16[2,16,16384]{2,1,0:T(8,128)(2,1)}, u32[]{:S(2)}) copy-start(bf16[2,16,16384]{2,1,0:T(8,128)(2,1)} %param.8) | copy-start | bytes 3145732
  54.9 209.1 %all-to-all-start = ((bf16[32,3,16384]{2,1,0:T(4,128)(2,1)}), bf16[32,3,16384]{2,1,0:T(4,128)(2,1)}, u32[]{:S(2)}, u32[]{:S(2)}) async-start(bf16[32,3,16384]{2,1,0:T(4,128)(2,1)} %broadcast_select_fusion), calls=%async_computation | async-start | bytes 8388608 | tf_op jit(solution)/shard_map/all_to_all | solution.py:51
  271.5 0.6 copy-start.2
  275.3 0.6 copy-start.4
  293.3 22.1 %all-to-all-start.2 = ((f32[32,1,3]{2,1,0:T(1,128)}), f32[32,1,3]{2,1,0:T(1,128)S(1)}, u32[]{:S(2)}, u32[]{:S(2)}) async-start(f32[32,1,3]{2,1,0:T(1,128)} %bitcast.85), calls=%async_computation.2 | async-start | bytes 32768 | tf_op jit(solution)/shard_map/all_to_all | solution.py:64
  315.4 16.2 %all-to-all-start.1 = ((f32[32,1,3]{2,1,0:T(1,128)}), f32[32,1,3]{2,1,0:T(1,128)S(1)}, u32[]{:S(2)}, u32[]{:S(2)}) async-start(f32[32,1,3]{2,1,0:T(1,128)} %bitcast.14), calls=%async_computation.1 | async-start | bytes 32768 | tf_op jit(solution)/shard_map/all_to_all | solution.py:63
  435.0 1.3 copy-start.6
  436.3 0.7 copy-start.5
  437.1 0.7 copy-start.3
where the time goes:
time: 442 us; the launch traced here: 441 us
  waiting for transfers between devices  200 us (45%)
  blocking collectives  125 us (28%)
  starting transfers between devices  40.5 us (9%)
  local copies, waits for them, and re-layouts  30.9 us (7%)
  other arithmetic  27.7 us (6%)
  matrix products  16.1 us (4%)
    all_to_all x1, waiting for transfers between devices, per_device(): lax.all_to_all(outgoing, 'pose', split_axis=0, concat_axis=0, tiled=True)  178 us
    pmax x1, blocking collectives, per_device(): overall_top = lax.pmax(group_top, 'cls')  30.9 us
    all_to_all x1, blocking collectives, per_device(): lax.all_to_all(slot_evidence, 'pose', split_axis=0, concat_axis=0, tiled=...  29.6 us
    psum x1, blocking collectives, per_device(): lax.psum(group_total * jnp.exp(group_top - overall_top), 'cls')  28.5 us
    all_to_all x1, starting transfers between devices, per_device(): lax.all_to_all(outgoing, 'pose', split_axis=0, concat_axis=0, tiled=True)  25.8 us
    all_gather x1, blocking collectives, per_device(): lax.all_gather(images, 'cls', axis=0, tiled=True)  18.3 us
    all_gather x1, blocking collectives, per_device(): lax.all_gather(significant, 'cls', axis=0, tiled=True)  17.3 us
    dot_general x4, matrix products, per_device(): lax.dot_general(rows, table, (((1,), (1,)), ((), ())), preferred_element_...  13.1 us
  transfers between devices with their start and end apart: 3, of which 3 were waited for; matrix products, arithmetic and copies ran while one was open for 2% of the time, Pallas kernels for 0%

commit v1 on v0

v1 whole, which is shorter than its diff:
```python
import jax
import jax.numpy as jnp
from jax import lax
from jax.experimental import pallas as pl
from jax.experimental.pallas import tpu as pltpu
from jax.sharding import Mesh, PartitionSpec as P

BF = jnp.bfloat16
F32 = jnp.float32
I32 = jnp.int32
NEG = -3.0e38

NX, NY, NZ, NC = 4, 4, 16, 2
NG = NX * NY
GR = 16
CAP = 3
BINS = 32
NT = 4
COEF = 8192
CH = COEF // NG
CW = 2 * CH
PAIR = 32
COMB = NT * PAIR
SLOTS = 2 * GR * CAP


def iota(shape, dim):
    return lax.broadcasted_iota(I32, shape, dim)


def nt_dot(a, b):
    return lax.dot_general(a, b, (((1,), (1,)), ((), ())), preferred_element_type=F32)


def nn_dot(a, b):
    return lax.dot_general(a, b, (((1,), (0,)), ((), ())), preferred_element_type=F32)


def vmem():
    return pl.BlockSpec(memory_space=pltpu.VMEM)


def smem():
    return pl.BlockSpec(memory_space=pltpu.SMEM)


def select_kernel(idx_ref, x_ref, out_ref, own_ref, scr):
    core = idx_ref[0]
    scr[...] = x_ref[...].astype(F32).reshape(2 * GR * 16, 128)
    member = scr[pl.ds(8, 2 * GR, stride=16), :]
    row = iota((32, 32), 0)
    col = iota((32, 32), 1)
    tri = jnp.where((row // GR == col // GR) & (col < row), 1.0, 0.0).astype(BF)
    rank = nn_dot(tri, member.astype(BF))
    both = (member + pltpu.roll(rank, 32, 1)).astype(BF)
    pick = (iota((128, 128), 1) == 2 * (iota((128, 128), 0) // 8) + core).astype(F32).astype(BF)
    mem = nt_dot(pick, member.astype(BF))
    rnk = nt_dot(pick, rank.astype(BF)).astype(I32)
    k = iota((128, 32), 0) % 8
    block = iota((128, 32), 1) // GR
    rnk = jnp.where(mem > 0.5, rnk + CAP * block, -1)
    rank_ok = (rnk >= CAP * block) & (rnk < CAP * block + CAP)
    rnk = jnp.where(rank_ok, rnk, -1)
    sel = jnp.where(rnk == k, 1.0, 0.0).astype(BF)
    for j in range(8):
        rows = scr[pl.ds(j, 2 * GR, stride=16), :].astype(BF)
        o = nn_dot(sel, rows)
        if j < 6:
            sel6 = jnp.where((k == 6) & (rnk == j), 1.0, 0.0).astype(BF)
            o = o + nn_dot(sel6, both)
        out_ref[:, j * 128 : (j + 1) * 128] = o.astype(BF)
    mine = iota((32, 128), 0) == core * GR + idx_ref[2]
    own = jnp.sum(jnp.where(mine, both.astype(F32), 0.0), axis=0, keepdims=True)
    own_ref[...] = jnp.broadcast_to(own, (8, 128))


def spread_kernel(y_ref, out_ref, scr, sem):
    s = iota((SLOTS, 128), 0)
    compact = jnp.where(iota((SLOTS, 128), 1) == (s // 6) * 8 + s % 6, 1.0, 0.0).astype(BF)
    scr[...] = nn_dot(compact, y_ref[...]).astype(BF)
    copies = [pltpu.make_async_copy(scr, out_ref.at[g], sem.at[g]) for g in range(NG)]
    for c in copies:
        c.start()
    for c in copies:
        c.wait()


def info_kernel(idx_ref, y_ref, own_ref, out_ref):
    s = iota((128, 128), 0)
    info = jnp.zeros((128, 128), F32)
    for j in range(6):
        hit = (iota((128, 128), 1) == (s // 6) * 8 + 6) & (s % 6 == j) & (s < SLOTS)
        info = info + nn_dot(
            jnp.where(hit, 1.0, 0.0).astype(BF), y_ref[:, j * 128 : (j + 1) * 128]
        )
    info = info.astype(BF)
    own = own_ref[...].astype(BF)
    z = iota((16, 128), 0)
    lane = iota((16, 128), 1)
    for c in range(2):
        pm = jnp.where(lane == 2 * z + c, 1.0, 0.0).astype(BF)
        pr = jnp.where(lane == 32 + 2 * z + c, 1.0, 0.0).astype(BF)
        out_ref[c] = nt_dot(pm, info)
        out_ref[2 + c] = nt_dot(pr, info)
        om = nt_dot(pm, own)[:, :1]
        orank = nt_dot(pr, own)[:, :1].astype(I32)
        out_ref[4 + c] = jnp.where((om > 0.5) & (lane == CAP * idx_ref[1] + orank), 1.0, 0.0)


def rotate_kernel(p_ref, c_ref, s_ref, out_ref):
    pr = p_ref[0].astype(F32)
    pi = p_ref[1].astype(F32)
    for t in range(NT):
        c = c_ref[t : t + 1, :]
        s = s_ref[t : t + 1, :]
        out_ref[0, t * PAIR : (t + 1) * PAIR, :CH] = (c * pr - s * pi).astype(BF)
        out_ref[0, t * PAIR : (t + 1) * PAIR, CH:] = (s * pr + c * pi).astype(BF)


def score_kernel(t_ref, r_ref, score_ref, lse_ref):
    acc = nt_dot(t_ref[0], r_ref[0])
    for g in range(1, NG):
        acc = acc + nt_dot(t_ref[g], r_ref[g])
    score_ref[...] = jnp.zeros((COMB, 128), F32)
    score_ref[:, :SLOTS] = acc
    sc = score_ref[...]
    top = jnp.max(sc, axis=0, keepdims=True)
    lse = top + jnp.log(jnp.sum(jnp.exp(sc - top), axis=0, keepdims=True))
    lse_ref[...] = jnp.broadcast_to(lse[None], (NC * NG, 1, 128))


def merge_kernel(l_ref, out_ref):
    parts = []
    for c in range(NC):
        v = l_ref[c * NG : (c + 1) * NG].reshape(NG, 128)
        top = jnp.max(v, axis=0, keepdims=True)
        parts.append(top + jnp.log(jnp.sum(jnp.exp(v - top), axis=0, keepdims=True)))
    both = jnp.concatenate(parts, axis=0)
    out_ref[...] = jnp.broadcast_to(both[None], (NZ, NC, 128))


def back_kernel(l_ref, info_ref, score_ref, r_ref, c_ref, s_ref, out_ref, ev_ref):
    lane3 = iota((NZ, 128), 1) % CAP
    sel, own = [], []
    for c in range(NC):
        level = l_ref[:, c, :]
        shift = info_ref[2 + c].astype(I32) - lane3
        v = level
        for d in (-2, -1, 1, 2):
            v = jnp.where(shift == d, pltpu.roll(level, (-d) % 128, 1), v)
        sel.append(jnp.where(info_ref[c] > 0.5, v, NEG))
        own.append(jnp.where(info_ref[4 + c] > 0.5, level, NEG))

    def lse(pair, axes):
        top = jnp.max(jnp.maximum(pair[0], pair[1]), axis=axes, keepdims=True)
        tot = sum(jnp.where(v > 0.5 * NEG, jnp.exp(v - top), 0.0) for v in pair)
        return top, jnp.sum(tot, axis=axes, keepdims=True)

    top, tot = lse(own, (0, 1))
    ev_ref[...] = jnp.broadcast_to(top + jnp.log(tot), (8, 128))
    top, tot = lse(sel, (0,))
    level = jnp.where(tot > 0.0, top + jnp.log(jnp.where(tot > 0.0, tot, 1.0)), 0.0)
    w = jnp.exp(score_ref[...] - level)[:, :SLOTS].astype(BF)
    for g in range(NG):
        part = nn_dot(w, r_ref[g])
        re = jnp.zeros((PAIR, CH), F32)
        im = jnp.zeros((PAIR, CH), F32)
        for t in range(NT):
            c = c_ref[t : t + 1, g * CH : (g + 1) * CH]
            s = s_ref[t : t + 1, g * CH : (g + 1) * CH]
            gr = part[t * PAIR : (t + 1) * PAIR, :CH]
            gi = part[t * PAIR : (t + 1) * PAIR, CH:]
            re = re + (c * gr + s * gi)
            im = im + (c * gi - s * gr)
        out_ref[:, g * CH : (g + 1) * CH] = re.astype(BF)
        out_ref[:, COEF + g * CH : COEF + (g + 1) * CH] = im.astype(BF)


def a2a(v, axes):
    return lax.all_to_all(v, axes, split_axis=0, concat_axis=0, tiled=True)


def per_device(images, significant, projections, phase):
    core = lax.axis_index("core")
    pose = lax.axis_index(("z", "core"))
    group = lax.axis_index(("x", "y"))
    idx = jnp.stack([core, pose, group]).astype(I32)

    chunks = images.reshape(2, NG, CH // 128, 128).transpose(1, 0, 2, 3).reshape(NG, 8, 128)
    lanes = jnp.arange(128, dtype=I32)
    member = jnp.any(significant.reshape(-1, 1) == lanes[None, :], axis=0).astype(BF)
    extra = jnp.where(jnp.arange(8)[:, None] == 0, member[None, :], jnp.zeros((), BF))
    first = jnp.concatenate([chunks, jnp.broadcast_to(extra[None], (NG, 8, 128))], axis=1)
    first = jnp.concatenate([first, first], axis=0)
    x1 = a2a(first, ("core", "x", "y"))

    cosv = jnp.cos(phase)
    sinv = jnp.sin(phase)
    proj = projections.reshape(PAIR, 2, COEF).transpose(1, 0, 2)
    table = pl.pallas_call(
        rotate_kernel,
        grid=(NG,),
        in_specs=[
            pl.BlockSpec((2, PAIR, CH), lambda g: (0, 0, g)),
            pl.BlockSpec((NT, CH), lambda g: (0, g)),
            pl.BlockSpec((NT, CH), lambda g: (0, g)),
        ],
        out_specs=pl.BlockSpec((1, COMB, CW), lambda g: (g, 0, 0)),
        out_shape=jax.ShapeDtypeStruct((NG, COMB, CW), BF),
        name="rotate",
    )(proj, cosv, sinv)

    picked, own = pl.pallas_call(
        select_kernel,
        in_specs=[smem(), vmem()],
        out_specs=[vmem(), vmem()],
        out_shape=[
            jax.ShapeDtypeStruct((NZ * 8, CW), BF),
            jax.ShapeDtypeStruct((8, 128), F32),
        ],
        scratch_shapes=[pltpu.VMEM((2 * GR * 16, 128), F32)],
        name="select",
    )(idx, x1)
    y2 = a2a(picked.reshape(NZ, 8, CW), "z").reshape(NZ * 8, CW)

    spread = pl.pallas_call(
        spread_kernel,
        in_specs=[vmem()],
        out_specs=pl.BlockSpec(memory_space=pl.ANY),
        out_shape=jax.ShapeDtypeStruct((NG, SLOTS, CW), BF),
        scratch_shapes=[pltpu.VMEM((SLOTS, CW), BF), pltpu.SemaphoreType.DMA((NG,))],
        name="spread",
    )(y2)
    rows = a2a(spread, ("x", "y"))
    info = pl.pallas_call(
        info_kernel,
        in_specs=[smem(), vmem(), vmem()],
        out_specs=vmem(),
        out_shape=jax.ShapeDtypeStruct((6, NZ, 128), F32),
        name="info",
    )(idx, y2, own)

    scores, lse = pl.pallas_call(
        score_kernel,
        in_specs=[vmem(), vmem()],
        out_specs=[vmem(), vmem()],
        out_shape=[
            jax.ShapeDtypeStruct((COMB, 128), F32),
            jax.ShapeDtypeStruct((NC * NG, 1, 128), F32),
        ],
        name="score",
    )(table, rows)
    l4 = a2a(lse, ("core", "x", "y"))
    merged = pl.pallas_call(
        merge_kernel,
        in_specs=[vmem()],
        out_specs=vmem(),
        out_shape=jax.ShapeDtypeStruct((NZ, NC, 128), F32),
        name="merge",
    )(l4)
    l5 = a2a(merged, "z")

    back, ev = pl.pallas_call(
        back_kernel,
        in_specs=[vmem()] * 6,
        out_specs=[vmem(), vmem()],
        out_shape=[
            jax.ShapeDtypeStruct((PAIR, 2 * COEF), BF),
            jax.ShapeDtypeStruct((8, 128), F32),
        ],
        name="back",
    )(l5, info, scores, rows, cosv, sinv)
    return back.reshape(projections.shape), ev[0, :1]


def solution(mesh):
    fine = Mesh(mesh.devices.reshape(NX, NY, NZ, NC), ("x", "y", "z", "core"))
    every = ("z", "core", "x", "y")
    cls = ("x", "y")
    pose = ("z", "core")
    return jax.shard_map(
        per_device,
        mesh=fine,
        in_specs=(P(every, None), P(every, None), P(cls, pose, None), P()),
        out_specs=(P(cls, pose, None), P(every)),
        check_vma=False,
    )
```

time: 442 us -> 155 us (0.35)
  waiting for transfers between devices: 200 us -> 34.6 us
  blocking collectives: 125 us -> 49 us
  Pallas kernels: 0 us -> 28.4 us
  other arithmetic: 27.7 us -> 3.08 us
  local copies, waits for them, and re-layouts: 30.9 us -> 11.2 us
  matrix products: 16.1 us -> 0 us
  starting transfers between devices: 40.5 us -> 26.5 us
    all_to_all x3, waiting for transfers between devices: 200 us -> 34.6 us  [a2a(): return lax.all_to_all(v, axes, split_axis=0, concat_axis=0, tiled=True)]
    all_gather x2 -> x0, blocking collectives: 35.7 us -> none  [the longest x1 18.3 us: per_device(): lax.all_gather(images, 'cls', axis=0, tiled=True)]
    pmax x1 -> x0, blocking collectives: 30.9 us -> none  [per_device(): overall_top = lax.pmax(group_top, 'cls')]
    psum x1 -> x0, blocking collectives: 28.5 us -> none  [per_device(): lax.psum(group_total * jnp.exp(group_top - overall_top), 'cls')]
    pallas_call x0 -> x7, Pallas kernels: none -> 28.4 us  [the longest x1 9.76 us: per_device(): pl.pallas_call(rotate_kernel, grid=(NG,), in_specs=[pl.BlockSpec((2, PAIR...]
    all_to_all x1 -> x2, blocking collectives: 29.6 us -> 49 us  [a2a(): return lax.all_to_all(v, axes, split_axis=0, concat_axis=0, tiled=True)]
    dot_general x8 -> x0, matrix products: 16.1 us -> none  [the longest x4 13.1 us: per_device(): lax.dot_general(rows, table, (((1,), (1,)), ((), ())), preferred_element_...]
    select_n x7 -> x1, other arithmetic: 15.8 us -> 0.07 us  [per_device(): jnp.where(jnp.arange(8)[:, None] == 0, member[None, :], jnp.zeros((), BF))]
  transfers between devices with their start and end apart: 3 -> 3, of which waited for: 3 -> 3; matrix products, arithmetic and copies ran while one was open for 2% -> 5% of each run, Pallas kernels for 0% -> 8%
where the time goes in v1:
time: 155 us; the launch traced here: 153 us
  blocking collectives  49 us (32%)
  waiting for transfers between devices  34.6 us (22%)
  Pallas kernels  28.4 us (18%)
  starting transfers between devices  26.5 us (17%)
  local copies, waits for them, and re-layouts  11.2 us (7%)
  other arithmetic  3.08 us (2%)
    all_to_all x2, blocking collectives, a2a(): return lax.all_to_all(v, axes, split_axis=0, concat_axis=0, tiled=True)  49 us
    all_to_all x3, waiting for transfers between devices, a2a(): return lax.all_to_all(v, axes, split_axis=0, concat_axis=0, tiled=True)  34.6 us
    all_to_all x3, starting transfers between devices, a2a(): return lax.all_to_all(v, axes, split_axis=0, concat_axis=0, tiled=True)  26.5 us
    pallas_call x1, Pallas kernels, per_device(): pl.pallas_call(rotate_kernel, grid=(NG,), in_specs=[pl.BlockSpec((2, PAIR...  9.76 us
    reshape x2, local copies, waits for them, and re-layouts, per_device(): proj = projections.reshape(PAIR, 2, COEF).transpose(1, 0, 2)  5.47 us
    pallas_call x1, Pallas kernels, per_device(): pl.pallas_call(score_kernel, in_specs=[vmem(), vmem()], out_specs=[vmem()...  5.08 us
    pallas_call x1, Pallas kernels, per_device(): pl.pallas_call(back_kernel, in_specs=[vmem()] * 6, out_specs=[vmem(), vme...  4.93 us
  transfers between devices with their start and end apart: 3, of which 3 were waited for; matrix products, arithmetic and copies ran while one was open for 5% of the time, Pallas kernels for 8%

profile of v1, /device:TPU:1, one launch (start us, length us, event | category | flops | bytes accessed | tf_op | source)
XLA Modules:
  0.0 153.4 jit_solution(8880721330118519715)
XLA Ops:
  0.6 0.7 fusion
  1.4 1.0 reduce
  2.4 0.1 broadcast_select_fusion
  2.5 0.7 maximum_maximum_fusion
  3.2 10.5 %all-to-all-start = ((bf16[32,16,128]{2,1,0:T(8,128)(2,1)}), bf16[32,16,128]{2,1,0:T(8,128)(2,1)S(1)}, u32[]{:S(2)}, u32[]{:S(2)}) async-start(bf16[32,16,128]{2,1,0:T(8,128)(2,1)} %maximum_maximum_fusion), calls=%async_computation | async-start | bytes 262144 | tf_op jit(solution)/shard_map/all_to_all | solution.py:180
  13.7 0.6 pad_add_fusion.idx_ref
  14.2 7.0 %all-to-all-done.x_ref = bf16[32,16,128]{2,1,0:T(8,128)(2,1)S(1)} async-done(((bf16[32,16,128]{2,1,0:T(8,128)(2,1)}), bf16[32,16,128]{2,1,0:T(8,128)(2,1)S(1)}, u32[]{:S(2)}, u32[]{:S(2)}) %all-to-all-start) | async-done | bytes 131104 | tf_op jit(solution)/shard_map/all_to_all | solution.py:180
  21.2 0.0 copy-start.1
  21.2 0.6 copy-done.1
  21.9 2.2 %select.1 = (bf16[128,1024]{1,0:T(8,128)(2,1)}, f32[8,128]{1,0:T(8,128)}) custom-call(s32[3]{0:T(128)} %pad_add_fusion.idx_ref, bf16[32,16,128]{2,1,0:T(8,128)(2,1)} %copy-done.1), custom_call_target="tpu_custom_call" | custom-call | tf_op jit(solution)/shard_map/select/pallas_call | solution.py:213
  24.0 26.9 %all_to_all.25 = bf16[16,8,1024]{2,1,0:T(8,128)(2,1)} all-to-all(bf16[16,8,1024]{2,1,0:T(8,128)(2,1)} %bitcast.18), channel_id=1, replica_groups=mesh['x'=4,'y'=4,'z'=16,'core'=2] {'z'}, dimensions={0} | all-to-all | bytes 524288 | tf_op jit(solution)/shard_map/all_to_all | solution.py:180
  51.0 3.0 %spread.1 = bf16[16,96,1024]{2,1,0:T(8,128)(2,1)} custom-call(bf16[128,1024]{1,0:T(8,128)(2,1)} %bitcast.16), custom_call_target="tpu_custom_call" | custom-call | tf_op jit(solution)/shard_map/spread/pallas_call | solution.py:226
  53.9 3.8 %all-to-all-start.2 = ((bf16[16,96,1024]{2,1,0:T(8,128)(2,1)}), bf16[16,96,1024]{2,1,0:T(8,128)(2,1)S(1)}, u32[]{:S(2)}, u32[]{:S(2)}) async-start(bf16[16,96,1024]{2,1,0:T(8,128)(2,1)} %spread.1), calls=%async_computation.2 | async-start | bytes 6291456 | tf_op jit(solution)/shard_map/all_to_all | solution.py:180
  57.7 0.0 copy-start.2
  57.7 2.7 %reshape.59 = bf16[32,2,8192]{2,1,0:T(2,128)(2,1)} reshape(bf16[2,16,16384]{2,1,0:T(8,128)(2,1)} %param.6) | data formatting | bytes 2097152 | tf_op jit(solution)/shard_map/reshape | solution.py:199
  60.3 2.8 %copy.12 = bf16[32,2,8192]{2,0,1:T(8,128)(2,1)} copy(bf16[32,2,8192]{2,1,0:T(2,128)(2,1)} %reshape.59) | data formatting | bytes 2097152 | tf_op jit(solution)/shard_map/reshape | solution.py:199
  63.2 0.0 copy-done.2
  63.2 1.6 %fusion.1 = (f32[4,8192]{1,0:T(4,128)}, f32[4,8192]{1,0:T(4,128)}) fusion(f32[4,8192]{1,0:T(4,128)S(1)} %copy-done.2), kind=kLoop, calls=%fused_computation.7 | loop fusion | bytes 393216 | tf_op jit(solution)/shard_map/sin | solution.py:198
  64.8 9.8 %rotate.1.t_ref = bf16[16,128,1024]{2,1,0:T(8,128)(2,1)} custom-call(bf16[2,32,8192]{2,1,0:T(8,128)(2,1)} %bitcast.15, f32[4,8192]{1,0:T(4,128)} %get-tuple-element.15.c_ref, f32[4,8192]{1,0:T(4,128)} %get-tuple-element.14.s_ref), custom_call_target="tpu_custom_call" | custom-call | tf_op jit(solution)/shard_map/rotate/pallas_call | solution.py:200
  74.5 18.3 %all-to-all-done.2.r_ref = bf16[16,96,1024]{2,1,0:T(8,128)(2,1)S(1)} async-done(((bf16[16,96,1024]{2,1,0:T(8,128)(2,1)}), bf16[16,96,1024]{2,1,0:T(8,128)(2,1)S(1)}, u32[]{:S(2)}, u32[]{:S(2)}) %all-to-all-start.2) | async-done | bytes 3145760 | tf_op jit(solution)/shard_map/all_to_all | solution.py:180
  92.8 0.0 copy-start
  92.8 1.7 %copy-done = bf16[16,96,1024]{2,1,0:T(8,128)(2,1)} copy-done((bf16[16,96,1024]{2,1,0:T(8,128)(2,1)}, bf16[16,96,1024]{2,1,0:T(8,128)(2,1)S(1)}, u32[]{:S(2)}) %copy-start) | copy-done | bytes 3145752
  94.5 5.1 %score.1 = (f32[128,128]{1,0:T(8,128)}, f32[32,1,128]{2,1,0:T(1,128)}) custom-call(bf16[16,128,1024]{2,1,0:T(8,128)(2,1)} %rotate.1.t_ref, bf16[16,96,1024]{2,1,0:T(8,128)(2,1)} %copy-done), custom_call_target="tpu_custom_call" | custom-call | tf_op jit(solution)/shard_map/score/pallas_call | solution.py:243
  99.6 22.1 %all_to_all.26.l_ref = f32[32,1,128]{2,1,0:T(1,128)} all-to-all(f32[32,1,128]{2,1,0:T(1,128)} %get-tuple-element.9), channel_id=1, replica_groups=mesh['x'=4,'y'=4,'z'=16,'core'=2] {'core','x','y'}, dimensions={0} | all-to-all | bytes 32768 | tf_op jit(solution)/shard_map/all_to_all | solution.py:180
  121.7 1.4 merge.1
  123.0 12.3 %all-to-all-start.4 = ((f32[16,2,128]{2,1,0:T(2,128)}), f32[16,2,128]{2,1,0:T(2,128)S(1)}, u32[]{:S(2)}, u32[]{:S(2)}) async-start(f32[16,2,128]{2,1,0:T(2,128)} %merge.1), calls=%async_computation.4 | async-start | bytes 32768 | tf_op jit(solution)/shard_map/all_to_all | solution.py:180
  135.3 2.1 %info.1.info_ref = f32[6,16,128]{2,1,0:T(8,128)} custom-call(s32[3]{0:T(128)} %pad_add_fusion.idx_ref, bf16[128,1024]{1,0:T(8,128)(2,1)} %bitcast.17, f32[8,128]{1,0:T(8,128)} %get-tuple-element.10.own_ref), custom_call_target="tpu_custom_call" | custom-call | tf_op jit(solution)/shard_map/info/pallas_call | solution.py:235
  137.4 9.3 %all-to-all-done.4.l_ref = f32[16,2,128]{2,1,0:T(2,128)S(1)} async-done(((f32[16,2,128]{2,1,0:T(2,128)}), f32[16,2,128]{2,1,0:T(2,128)S(1)}, u32[]{:S(2)}, u32[]{:S(2)}) %all-to-all-start.4) | async-done | bytes 16416 | tf_op jit(solution)/shard_map/all_to_all | solution.py:180
  146.7 0.0 copy-start.3
  146.7 0.6 copy-done.3
  147.3 4.9 %back.1 = (bf16[32,16384]{1,0:T(8,128)(2,1)}, f32[8,128]{1,0:T(8,128)}) custom-call(f32[16,2,128]{2,1,0:T(2,128)} %copy-done.3, f32[6,16,128]{2,1,0:T(8,128)} %info.1.info_ref, f32[128,128]{1,0:T(8,128)} %get-tuple-element.11.score_ref, bf16[16,96,1024]{2,1,0:T(8,128)(2,1)} %copy-done, f32[4,8192]{1,0:T(4,128)} %get-tuple-element.15.c_ref, ...), custom_call_target="tpu_custom_call" | custom-call | tf_op jit(solution)/shard_map/back/pallas_call | solution.py:263
  152.2 1.2 slice.3
  (4 shorter events, 0.0 us)
Async XLA Ops:
  3.2 18.0 %all-to-all-start = ((bf16[32,16,128]{2,1,0:T(8,128)(2,1)}), bf16[32,16,128]{2,1,0:T(8,128)(2,1)S(1)}, u32[]{:S(2)}, u32[]{:S(2)}) async-start(bf16[32,16,128]{2,1,0:T(8,128)(2,1)} %maximum_maximum_fusion), calls=%async_computation | async-start | bytes 262144 | tf_op jit(solution)/shard_map/all_to_all | solution.py:180
  21.2 0.7 copy-start.1
  53.9 38.9 %all-to-all-start.2 = ((bf16[16,96,1024]{2,1,0:T(8,128)(2,1)}), bf16[16,96,1024]{2,1,0:T(8,128)(2,1)S(1)}, u32[]{:S(2)}, u32[]{:S(2)}) async-start(bf16[16,96,1024]{2,1,0:T(8,128)(2,1)} %spread.1), calls=%async_computation.2 | async-start | bytes 6291456 | tf_op jit(solution)/shard_map/all_to_all | solution.py:180
  57.7 5.5 %copy-start.2 = (f32[4,8192]{1,0:T(4,128)S(1)}, f32[4,8192]{1,0:T(4,128)}, u32[]{:S(2)}) copy-start(f32[4,8192]{1,0:T(4,128)} %param.7) | copy-start | bytes 393220
  92.8 1.7 %copy-start = (bf16[16,96,1024]{2,1,0:T(8,128)(2,1)}, bf16[16,96,1024]{2,1,0:T(8,128)(2,1)S(1)}, u32[]{:S(2)}) copy-start(bf16[16,96,1024]{2,1,0:T(8,128)(2,1)S(1)} %all-to-all-done.2.r_ref) | copy-start | bytes 9437188
  123.0 23.7 %all-to-all-start.4 = ((f32[16,2,128]{2,1,0:T(2,128)}), f32[16,2,128]{2,1,0:T(2,128)S(1)}, u32[]{:S(2)}, u32[]{:S(2)}) async-start(f32[16,2,128]{2,1,0:T(2,128)} %merge.1), calls=%async_computation.4 | async-start | bytes 32768 | tf_op jit(solution)/shard_map/all_to_all | solution.py:180
  146.7 0.6 copy-start.3

commit v2 on v1

--- a/solution.py
+++ b/solution.py
@@ -40,8 +40,30 @@
     return pl.BlockSpec(memory_space=pltpu.VMEM)
 
 
+def anywhere():
+    return pl.BlockSpec(memory_space=pltpu.HBM)
+
+
 def smem():
     return pl.BlockSpec(memory_space=pltpu.SMEM)
+
+
+def prepare_kernel(sig_ref, x_ref, out_ref, scr):
+    lane = iota((1, 128), 1)
+    hit = (lane == sig_ref[0, 0]) | (lane == sig_ref[0, 1]) | (lane == sig_ref[0, 2])
+    member = jnp.where(hit, 1.0, 0.0)
+    scr[...] = jnp.zeros((NG * 16, 128), F32)
+    scr[pl.ds(8, NG, stride=16), :] = jnp.broadcast_to(member, (NG, 128))
+    x = x_ref[...].astype(F32)
+    for g in range(NG):
+        for j in range(CH // 128):
+            at = g * CH + j * 128
+            scr[g * 16 + j : g * 16 + j + 1, :] = x[:, at : at + 128]
+            at = at + COEF
+            scr[g * 16 + 4 + j : g * 16 + 5 + j, :] = x[:, at : at + 128]
+    v = scr[...].reshape(NG, 16, 128).astype(BF)
+    out_ref[:NG] = v
+    out_ref[NG:] = v
 
 
 def select_kernel(idx_ref, x_ref, out_ref, own_ref, scr):
@@ -108,19 +130,25 @@
 
 
 def rotate_kernel(p_ref, c_ref, s_ref, out_ref):
-    pr = p_ref[0].astype(F32)
-    pi = p_ref[1].astype(F32)
-    for t in range(NT):
-        c = c_ref[t : t + 1, :]
-        s = s_ref[t : t + 1, :]
-        out_ref[0, t * PAIR : (t + 1) * PAIR, :CH] = (c * pr - s * pi).astype(BF)
-        out_ref[0, t * PAIR : (t + 1) * PAIR, CH:] = (s * pr + c * pi).astype(BF)
-
-
-def score_kernel(t_ref, r_ref, score_ref, lse_ref):
-    acc = nt_dot(t_ref[0], r_ref[0])
-    for g in range(1, NG):
-        acc = acc + nt_dot(t_ref[g], r_ref[g])
+    for g in range(NG):
+        lo = g * CH
+        pr = p_ref[:, lo : lo + CH].astype(F32)
+        pi = p_ref[:, COEF + lo : COEF + lo + CH].astype(F32)
+        for t in range(NT):
+            c = c_ref[t : t + 1, lo : lo + CH]
+            s = s_ref[t : t + 1, lo : lo + CH]
+            out_ref[g, t * PAIR : (t + 1) * PAIR, :CH] = (c * pr - s * pi).astype(BF)
+            out_ref[g, t * PAIR : (t + 1) * PAIR, CH:] = (s * pr + c * pi).astype(BF)
+
+
+def score_kernel(t_ref, r_ref, score_ref, lse_ref, scr, sem):
+    copies = [pltpu.make_async_copy(t_ref.at[g], scr.at[g], sem.at[g]) for g in range(NG)]
+    for c in copies:
+        c.start()
+    acc = jnp.zeros((COMB, SLOTS), F32)
+    for g in range(NG):
+        copies[g].wait()
+        acc = acc + nt_dot(scr[g], r_ref[g])
     score_ref[...] = jnp.zeros((COMB, 128), F32)
     score_ref[:, :SLOTS] = acc
     sc = score_ref[...]
@@ -139,7 +167,15 @@
     out_ref[...] = jnp.broadcast_to(both[None], (NZ, NC, 128))
 
 
-def back_kernel(l_ref, info_ref, score_ref, r_ref, c_ref, s_ref, out_ref, ev_ref):
+def back_kernel(
+    l_ref, info_ref, score_ref, r_ref, cos_ref, sin_ref, out_ref, ev_ref, c_ref, s_ref, sem
+):
+    copies = [
+        pltpu.make_async_copy(cos_ref, c_ref, sem.at[0]),
+        pltpu.make_async_copy(sin_ref, s_ref, sem.at[1]),
+    ]
+    for c in copies:
+        c.start()
     lane3 = iota((NZ, 128), 1) % CAP
     sel, own = [], []
     for c in range(NC):
@@ -148,19 +184,22 @@
         v = level
         for d in (-2, -1, 1, 2):
             v = jnp.where(shift == d, pltpu.roll(level, (-d) % 128, 1), v)
-        sel.append(jnp.where(info_ref[c] > 0.5, v, NEG))
-        own.append(jnp.where(info_ref[4 + c] > 0.5, level, NEG))
+        sel.append((info_ref[c] > 0.5, v))
+        own.append((info_ref[4 + c] > 0.5, level))
 
     def lse(pair, axes):
-        top = jnp.max(jnp.maximum(pair[0], pair[1]), axis=axes, keepdims=True)
-        tot = sum(jnp.where(v > 0.5 * NEG, jnp.exp(v - top), 0.0) for v in pair)
+        a, b = (jnp.where(m, v, NEG) for m, v in pair)
+        top = jnp.max(jnp.maximum(a, b), axis=axes, keepdims=True)
+        tot = sum(jnp.where(m, jnp.exp(v - top), 0.0) for m, v in pair)
         return top, jnp.sum(tot, axis=axes, keepdims=True)
 
     top, tot = lse(own, (0, 1))
-    ev_ref[...] = jnp.broadcast_to(top + jnp.log(tot), (8, 128))
+    ev_ref[...] = top + jnp.log(tot)
     top, tot = lse(sel, (0,))
     level = jnp.where(tot > 0.0, top + jnp.log(jnp.where(tot > 0.0, tot, 1.0)), 0.0)
     w = jnp.exp(score_ref[...] - level)[:, :SLOTS].astype(BF)
+    for c in copies:
+        c.wait()
     for g in range(NG):
         part = nn_dot(w, r_ref[g])
         re = jnp.zeros((PAIR, CH), F32)
@@ -180,97 +219,112 @@
     return lax.all_to_all(v, axes, split_axis=0, concat_axis=0, tiled=True)
 
 
+def call(kernel, name, operands, outs, near=(), far=(), away=(), scalars=0, scratch=()):
+    operands = [
+        pltpu.with_memory_space_constraint(v, pltpu.VMEM if n in near else pltpu.HBM)
+        if n in near or n in far
+        else v
+        for n, v in enumerate(operands)
+    ]
+    return pl.pallas_call(
+        kernel,
+        in_specs=[
+            smem() if n < scalars else anywhere() if n in far else vmem()
+            for n in range(len(operands))
+        ],
+        out_specs=[anywhere() if n in away else vmem() for n in range(len(outs))],
+        out_shape=list(outs),
+        scratch_shapes=scratch,
+        compiler_params=pltpu.CompilerParams(vmem_limit_bytes=16 << 20),
+        name=name,
+    )(*operands)
+
+
 def per_device(images, significant, projections, phase):
     core = lax.axis_index("core")
     pose = lax.axis_index(("z", "core"))
     group = lax.axis_index(("x", "y"))
     idx = jnp.stack([core, pose, group]).astype(I32)
 
-    chunks = images.reshape(2, NG, CH // 128, 128).transpose(1, 0, 2, 3).reshape(NG, 8, 128)
-    lanes = jnp.arange(128, dtype=I32)
-    member = jnp.any(significant.reshape(-1, 1) == lanes[None, :], axis=0).astype(BF)
-    extra = jnp.where(jnp.arange(8)[:, None] == 0, member[None, :], jnp.zeros((), BF))
-    first = jnp.concatenate([chunks, jnp.broadcast_to(extra[None], (NG, 8, 128))], axis=1)
-    first = jnp.concatenate([first, first], axis=0)
+    (first,) = call(
+        prepare_kernel,
+        "prepare",
+        [significant, images],
+        [pltpu.VMEM((NC * NG, 16, 128), BF)],
+        scalars=1,
+        scratch=[pltpu.VMEM((NG * 16, 128), F32)],
+    )
     x1 = a2a(first, ("core", "x", "y"))
 
     cosv = jnp.cos(phase)
     sinv = jnp.sin(phase)
-    proj = projections.reshape(PAIR, 2, COEF).transpose(1, 0, 2)
-    table = pl.pallas_call(
+    (table,) = call(
         rotate_kernel,
-        grid=(NG,),
-        in_specs=[
-            pl.BlockSpec((2, PAIR, CH), lambda g: (0, 0, g)),
-            pl.BlockSpec((NT, CH), lambda g: (0, g)),
-            pl.BlockSpec((NT, CH), lambda g: (0, g)),
+        "rotate",
+        [projections.reshape(PAIR, 2 * COEF), cosv, sinv],
+        [pltpu.HBM((NG, COMB, CW), BF)],
+    )
+
+    picked, own = call(
+        select_kernel,
+        "select",
+        [idx, x1],
+        [pltpu.VMEM((NZ * 8, CW), BF), pltpu.HBM((8, 128), F32)],
+        near=(1,),
+        scalars=1,
+        scratch=[pltpu.VMEM((2 * GR * 16, 128), F32)],
+    )
+    y2 = a2a(picked.reshape(NZ, 8, CW), "z").reshape(NZ * 8, CW)
+
+    (spread,) = call(
+        spread_kernel,
+        "spread",
+        [y2],
+        [pltpu.HBM((NG, SLOTS, CW), BF)],
+        near=(0,),
+        away=(0,),
+        scratch=[pltpu.VMEM((SLOTS, CW), BF), pltpu.SemaphoreType.DMA((NG,))],
+    )
+    rows = a2a(spread, ("x", "y"))
+    (info,) = call(
+        info_kernel,
+        "info",
+        [idx, y2, own],
+        [pltpu.VMEM((6, NZ, 128), F32)],
+        near=(1,),
+        scalars=1,
+    )
+    table, info = lax.optimization_barrier((table, info))
+
+    scores, lse = call(
+        score_kernel,
+        "score",
+        [table, rows],
+        [pltpu.VMEM((COMB, 128), F32), pltpu.VMEM((NC * NG, 1, 128), F32)],
+        near=(1,),
+        far=(0,),
+        scratch=[pltpu.VMEM((NG, COMB, CW), BF), pltpu.SemaphoreType.DMA((NG,))],
+    )
+    l4 = a2a(lse, ("core", "x", "y"))
+    (merged,) = call(
+        merge_kernel, "merge", [l4], [pltpu.VMEM((NZ, NC, 128), F32)], near=(0,)
+    )
+    l5 = a2a(merged, "z")
+
+    back, ev = call(
+        back_kernel,
+        "back",
+        [l5, info, scores, rows, cosv, sinv],
+        [pltpu.HBM((PAIR, 2 * COEF), BF), pltpu.HBM((1, 1), F32)],
+        near=(0, 1, 2, 3),
+        far=(4, 5),
+        scratch=[
+            pltpu.VMEM((NT, COEF), F32),
+            pltpu.VMEM((NT, COEF), F32),
+            pltpu.SemaphoreType.DMA((2,)),
         ],
-        out_specs=pl.BlockSpec((1, COMB, CW), lambda g: (g, 0, 0)),
-        out_shape=jax.ShapeDtypeStruct((NG, COMB, CW), BF),
-        name="rotate",
-    )(proj, cosv, sinv)
-
-    picked, own = pl.pallas_call(
-        select_kernel,
-        in_specs=[smem(), vmem()],
-        out_specs=[vmem(), vmem()],
-        out_shape=[
-            jax.ShapeDtypeStruct((NZ * 8, CW), BF),
-            jax.ShapeDtypeStruct((8, 128), F32),
-        ],
-        scratch_shapes=[pltpu.VMEM((2 * GR * 16, 128), F32)],
-        name="select",
-    )(idx, x1)
-    y2 = a2a(picked.reshape(NZ, 8, CW), "z").reshape(NZ * 8, CW)
-
-    spread = pl.pallas_call(
-        spread_kernel,
-        in_specs=[vmem()],
-        out_specs=pl.BlockSpec(memory_space=pl.ANY),
-        out_shape=jax.ShapeDtypeStruct((NG, SLOTS, CW), BF),
-        scratch_shapes=[pltpu.VMEM((SLOTS, CW), BF), pltpu.SemaphoreType.DMA((NG,))],
-        name="spread",
-    )(y2)
-    rows = a2a(spread, ("x", "y"))
-    info = pl.pallas_call(
-        info_kernel,
-        in_specs=[smem(), vmem(), vmem()],
-        out_specs=vmem(),
-        out_shape=jax.ShapeDtypeStruct((6, NZ, 128), F32),
-        name="info",
-    )(idx, y2, own)
-
-    scores, lse = pl.pallas_call(
-        score_kernel,
-        in_specs=[vmem(), vmem()],
-        out_specs=[vmem(), vmem()],
-        out_shape=[
-            jax.ShapeDtypeStruct((COMB, 128), F32),
-            jax.ShapeDtypeStruct((NC * NG, 1, 128), F32),
-        ],
-        name="score",
-    )(table, rows)
-    l4 = a2a(lse, ("core", "x", "y"))
-    merged = pl.pallas_call(
-        merge_kernel,
-        in_specs=[vmem()],
-        out_specs=vmem(),
-        out_shape=jax.ShapeDtypeStruct((NZ, NC, 128), F32),
-        name="merge",
-    )(l4)
-    l5 = a2a(merged, "z")
-
-    back, ev = pl.pallas_call(
-        back_kernel,
-        in_specs=[vmem()] * 6,
-        out_specs=[vmem(), vmem()],
-        out_shape=[
-            jax.ShapeDtypeStruct((PAIR, 2 * COEF), BF),
-            jax.ShapeDtypeStruct((8, 128), F32),
-        ],
-        name="back",
-    )(l5, info, scores, rows, cosv, sinv)
-    return back.reshape(projections.shape), ev[0, :1]
+    )
+    return back.reshape(projections.shape), ev.reshape(1)
 
 
 def solution(mesh):

time: 155 us -> 144 us (0.929)
  blocking collectives: 49 us -> 71.9 us
  starting transfers between devices: 26.5 us -> 14.2 us
  Pallas kernels: 28.4 us -> 16.9 us
  local copies, waits for them, and re-layouts: 11.2 us -> 5.24 us
  other arithmetic: 3.08 us -> 0.08 us
    all_to_all x2 -> x3, blocking collectives: 49 us -> 71.9 us  [a2a(): return lax.all_to_all(v, axes, split_axis=0, concat_axis=0, tiled=True)]
    all_to_all x3 -> x2, starting transfers between devices: 26.5 us -> 14.2 us  [a2a(): return lax.all_to_all(v, axes, split_axis=0, concat_axis=0, tiled=True)]
    pallas_call x7 -> x8, Pallas kernels: 28.4 us -> 16.9 us  [call(): pl.pallas_call(kernel, in_specs=[smem() if n < scalars else anywhere() if...]
    reshape x3 -> x0, local copies, waits for them, and re-layouts: 5.49 us -> none  [the longest x2 5.47 us: per_device(): proj = projections.reshape(PAIR, 2, COEF).transpose(1, 0, 2)]
    unnamed x8 -> x16, local copies, waits for them, and re-layouts: 2.92 us -> 3.45 us
    all_to_all x3 -> x2, waiting for transfers between devices: 34.6 us -> 34.8 us  [a2a(): return lax.all_to_all(v, axes, split_axis=0, concat_axis=0, tiled=True)]
  transfers between devices with their start and end apart: 3 -> 2, of which waited for: 3 -> 2; matrix products, arithmetic and copies ran while one was open for 5% -> 1% of each run, Pallas kernels for 8% -> 3%
where the time goes in v2:
time: 144 us
  blocking collectives  71.9 us (50%)
  waiting for transfers between devices  34.8 us (24%)
  Pallas kernels  16.9 us (12%)
  starting transfers between devices  14.2 us (10%)
  local copies, waits for them, and re-layouts  5.24 us (4%)
    all_to_all x3, blocking collectives, a2a(): return lax.all_to_all(v, axes, split_axis=0, concat_axis=0, tiled=True)  71.9 us
    all_to_all x2, waiting for transfers between devices, a2a(): return lax.all_to_all(v, axes, split_axis=0, concat_axis=0, tiled=True)  34.8 us
    pallas_call x8, Pallas kernels, call(): pl.pallas_call(kernel, in_specs=[smem() if n < scalars else anywhere() if...  16.9 us
    all_to_all x2, starting transfers between devices, a2a(): return lax.all_to_all(v, axes, split_axis=0, concat_axis=0, tiled=True)  14.2 us
    unnamed x16, local copies, waits for them, and re-layouts  3.45 us
  transfers between devices with their start and end apart: 2, of which 2 were waited for; matrix products, arithmetic and copies ran while one was open for 1% of the time, Pallas kernels for 3%

profile of v2, /device:TPU:1, one launch (start us, length us, event | category | flops | bytes accessed | tf_op | source)
XLA Modules:
  0.0 143.9 jit_solution(9606708958925979879)
XLA Ops:
  0.6 0.0 copy-start.5
  0.6 0.8 copy-done.5
  1.5 0.0 copy-start.7
  1.5 0.7 copy-done.7
  2.1 1.3 prepare.1
  3.4 10.5 %all-to-all-start = ((bf16[32,16,128]{2,1,0:T(8,128)(2,1)}), bf16[32,16,128]{2,1,0:T(8,128)(2,1)S(1)}, u32[]{:S(2)}, u32[]{:S(2)}) async-start(bf16[32,16,128]{2,1,0:T(8,128)(2,1)} %prepare.1), calls=%async_computation | async-start | bytes 262144 | tf_op jit(solution)/shard_map/all_to_all | solution.py:219
  13.9 0.1 pad_add_fusion.idx_ref
  13.9 7.5 %all-to-all-done.x_ref = bf16[32,16,128]{2,1,0:T(8,128)(2,1)S(1)} async-done(((bf16[32,16,128]{2,1,0:T(8,128)(2,1)}), bf16[32,16,128]{2,1,0:T(8,128)(2,1)S(1)}, u32[]{:S(2)}, u32[]{:S(2)}) %all-to-all-start) | async-done | bytes 131104 | tf_op jit(solution)/shard_map/all_to_all | solution.py:219
  21.4 1.4 select.1
  22.8 26.6 %all_to_all.25 = bf16[16,8,1024]{2,1,0:T(8,128)(2,1)S(1)} all-to-all(bf16[16,8,1024]{2,1,0:T(8,128)(2,1)S(1)} %bitcast.11), channel_id=1, replica_groups=mesh['x'=4,'y'=4,'z'=16,'core'=2] {'z'}, dimensions={0} | all-to-all | bytes 524288 | tf_op jit(solution)/shard_map/all_to_all | solution.py:219
  49.4 2.0 %spread.1 = bf16[16,96,1024]{2,1,0:T(8,128)(2,1)} custom-call(bf16[128,1024]{1,0:T(8,128)(2,1)S(1)} %bitcast.8), custom_call_target="tpu_custom_call" | custom-call | tf_op jit(solution)/shard_map/spread/pallas_call | solution.py:229
  51.4 3.8 %all-to-all-start.2 = ((bf16[16,96,1024]{2,1,0:T(8,128)(2,1)}), bf16[16,96,1024]{2,1,0:T(8,128)(2,1)S(1)}, u32[]{:S(2)}, u32[]{:S(2)}) async-start(bf16[16,96,1024]{2,1,0:T(8,128)(2,1)} %spread.1), calls=%async_computation.2 | async-start | bytes 6291456 | tf_op jit(solution)/shard_map/all_to_all | solution.py:219
  55.2 0.0 copy-start.6
  55.2 1.8 %fusion = (f32[4,8192]{1,0:T(4,128)S(1)}, f32[4,8192]{1,0:T(4,128)S(1)}) fusion(f32[4,8192]{1,0:T(4,128)} %param.7), kind=kLoop, calls=%fused_computation.1 | loop fusion | bytes 393216 | tf_op jit(solution)/shard_map/sin | solution.py:260
  57.0 0.0 copy-start.1
  57.0 0.0 copy-start
  57.0 0.0 copy-start.2
  57.0 1.3 copy-done.2
  58.3 3.0 %rotate.1.t_ref = bf16[16,128,1024]{2,1,0:T(8,128)(2,1)} custom-call(bf16[32,16384]{1,0:T(8,128)(2,1)S(1)} %bitcast.10, f32[4,8192]{1,0:T(4,128)S(1)} %get-tuple-element.19.c_ref.cos_ref, f32[4,8192]{1,0:T(4,128)S(1)} %get-tuple-element.18.s_ref.sin_ref), custom_call_target="tpu_custom_call" | custom-call | tf_op jit(solution)/shard_map/rotate/pallas_call | solution.py:229
  61.3 0.0 copy-done.1
  61.3 0.0 copy-done.6
  61.3 1.0 info.1.info_ref
  62.4 0.0 copy-start.3
  62.4 0.6 copy-done.3
  63.0 27.3 %all-to-all-done.2.r_ref = bf16[16,96,1024]{2,1,0:T(8,128)(2,1)S(1)} async-done(((bf16[16,96,1024]{2,1,0:T(8,128)(2,1)}), bf16[16,96,1024]{2,1,0:T(8,128)(2,1)S(1)}, u32[]{:S(2)}, u32[]{:S(2)}) %all-to-all-start.2) | async-done | bytes 3145760 | tf_op jit(solution)/shard_map/all_to_all | solution.py:219
  90.3 0.0 copy-start.4
  90.3 4.0 %score.1 = (f32[128,128]{1,0:T(8,128)S(1)}, f32[32,1,128]{2,1,0:T(1,128)S(1)}) custom-call(bf16[16,128,1024]{2,1,0:T(8,128)(2,1)} %rotate.1.t_ref, bf16[16,96,1024]{2,1,0:T(8,128)(2,1)S(1)} %all-to-all-done.2.r_ref), custom_call_target="tpu_custom_call" | custom-call | tf_op jit(solution)/shard_map/score/pallas_call | solution.py:229
  94.3 0.0 copy-done
  94.4 21.9 %all_to_all.26.l_ref = f32[32,1,128]{2,1,0:T(1,128)S(1)} all-to-all(f32[32,1,128]{2,1,0:T(1,128)S(1)} %get-tuple-element.13), channel_id=1, replica_groups=mesh['x'=4,'y'=4,'z'=16,'core'=2] {'core','x','y'}, dimensions={0} | all-to-all | bytes 32768 | tf_op jit(solution)/shard_map/all_to_all | solution.py:219
  116.3 23.5 %all_to_all.27.l_ref = f32[16,2,128]{2,1,0:T(2,128)S(1)} all-to-all(f32[16,2,128]{2,1,0:T(2,128)S(1)} %merge.1), channel_id=1, replica_groups=mesh['x'=4,'y'=4,'z'=16,'core'=2] {'z'}, dimensions={0} | all-to-all | bytes 32768 | tf_op jit(solution)/shard_map/all_to_all | solution.py:219
  139.7 0.0 copy-done.4
  139.7 4.2 %back.1 = (bf16[32,16384]{1,0:T(8,128)(2,1)}, f32[1,1]{1,0:T(1,128)}) custom-call(f32[16,2,128]{2,1,0:T(2,128)S(1)} %all_to_all.27.l_ref, f32[6,16,128]{2,1,0:T(8,128)S(1)} %copy-done.4, f32[128,128]{1,0:T(8,128)S(1)} %get-tuple-element.15.score_ref, bf16[16,96,1024]{2,1,0:T(8,128)(2,1)S(1)} %all-to-all-done.2.r_ref, f32[4,8192]{1,0:T(4,128)} %copy-done.1, ...), custom_call_target="tpu_custom_call" | custom-call | tf_op jit(solution)/shard_map/back/pallas_call | solution.py:229
  (1 shorter events, 0.0 us)
Async XLA Ops:
  0.6 0.8 copy-start.5
  1.5 0.7 copy-start.7
  3.4 18.0 %all-to-all-start = ((bf16[32,16,128]{2,1,0:T(8,128)(2,1)}), bf16[32,16,128]{2,1,0:T(8,128)(2,1)S(1)}, u32[]{:S(2)}, u32[]{:S(2)}) async-start(bf16[32,16,128]{2,1,0:T(8,128)(2,1)} %prepare.1), calls=%async_computation | async-start | bytes 262144 | tf_op jit(solution)/shard_map/all_to_all | solution.py:219
  51.4 38.9 %all-to-all-start.2 = ((bf16[16,96,1024]{2,1,0:T(8,128)(2,1)}), bf16[16,96,1024]{2,1,0:T(8,128)(2,1)S(1)}, u32[]{:S(2)}, u32[]{:S(2)}) async-start(bf16[16,96,1024]{2,1,0:T(8,128)(2,1)} %spread.1), calls=%async_computation.2 | async-start | bytes 6291456 | tf_op jit(solution)/shard_map/all_to_all | solution.py:219
  55.2 6.1 %copy-start.6 = (f32[8,128]{1,0:T(8,128)S(1)}, f32[8,128]{1,0:T(8,128)}, u32[]{:S(2)}) copy-start(f32[8,128]{1,0:T(8,128)} %get-tuple-element.11.own_ref) | copy-start | bytes 12292
  57.0 4.3 %copy-start.1 = (f32[4,8192]{1,0:T(4,128)}, f32[4,8192]{1,0:T(4,128)S(1)}, u32[]{:S(2)}) copy-start(f32[4,8192]{1,0:T(4,128)S(1)} %get-tuple-element.19.c_ref.cos_ref) | copy-start | bytes 393220
  57.0 37.4 %copy-start = (f32[4,8192]{1,0:T(4,128)}, f32[4,8192]{1,0:T(4,128)S(1)}, u32[]{:S(2)}) copy-start(f32[4,8192]{1,0:T(4,128)S(1)} %get-tuple-element.18.s_ref.sin_ref) | copy-start | bytes 393220
  57.0 1.3 copy-start.2
  62.4 0.6 copy-start.3
  90.3 49.4 %copy-start.4 = (f32[6,16,128]{2,1,0:T(8,128)S(1)}, f32[6,16,128]{2,1,0:T(8,128)}, u32[]{:S(2)}) copy-start(f32[6,16,128]{2,1,0:T(8,128)} %copy-done.3) | copy-start | bytes 147460

commit v3 on v2

--- a/solution.py
+++ b/solution.py
@@ -22,6 +22,12 @@
 PAIR = 32
 COMB = NT * PAIR
 SLOTS = 2 * GR * CAP
+
+FIRST_Z = 8
+PLANE = [((i // NY + 2) % NX) * NY + (i % NY + 2) % NY for i in range(NG)]
+ALONG_Z = [[(i + FIRST_Z) % NZ for i in range(NZ)]]
+IN_PLANE = [PLANE]
+IN_CHIPS = [PLANE + [NG + g for g in PLANE]]
 
 
 def iota(shape, dim):
@@ -75,7 +81,8 @@
     tri = jnp.where((row // GR == col // GR) & (col < row), 1.0, 0.0).astype(BF)
     rank = nn_dot(tri, member.astype(BF))
     both = (member + pltpu.roll(rank, 32, 1)).astype(BF)
-    pick = (iota((128, 128), 1) == 2 * (iota((128, 128), 0) // 8) + core).astype(F32).astype(BF)
+    to_z = (iota((128, 128), 0) // 8 + FIRST_Z) % NZ
+    pick = (iota((128, 128), 1) == 2 * to_z + core).astype(F32).astype(BF)
     mem = nt_dot(pick, member.astype(BF))
     rnk = nt_dot(pick, rank.astype(BF)).astype(I32)
     k = iota((128, 32), 0) % 8
@@ -117,7 +124,7 @@
         )
     info = info.astype(BF)
     own = own_ref[...].astype(BF)
-    z = iota((16, 128), 0)
+    z = (iota((16, 128), 0) + FIRST_Z) % NZ
     lane = iota((16, 128), 1)
     for c in range(2):
         pm = jnp.where(lane == 2 * z + c, 1.0, 0.0).astype(BF)
@@ -215,8 +222,10 @@
         out_ref[:, COEF + g * CH : COEF + (g + 1) * CH] = im.astype(BF)
 
 
-def a2a(v, axes):
-    return lax.all_to_all(v, axes, split_axis=0, concat_axis=0, tiled=True)
+def a2a(v, axes, order):
+    return lax.all_to_all(
+        v, axes, split_axis=0, concat_axis=0, tiled=True, axis_index_groups=order
+    )
 
 
 def call(kernel, name, operands, outs, near=(), far=(), away=(), scalars=0, scratch=()):
@@ -242,9 +251,11 @@
 
 def per_device(images, significant, projections, phase):
     core = lax.axis_index("core")
-    pose = lax.axis_index(("z", "core"))
-    group = lax.axis_index(("x", "y"))
-    idx = jnp.stack([core, pose, group]).astype(I32)
+    z = lax.axis_index("z")
+    block = 2 * ((z - FIRST_Z) % NZ) + core
+    x, y = lax.axis_index("x"), lax.axis_index("y")
+    place = ((x + 2) % NX) * NY + (y + 2) % NY
+    idx = jnp.stack([core, block, place]).astype(I32)
 
     (first,) = call(
         prepare_kernel,
@@ -254,7 +265,7 @@
         scalars=1,
         scratch=[pltpu.VMEM((NG * 16, 128), F32)],
     )
-    x1 = a2a(first, ("core", "x", "y"))
+    x1 = a2a(first, ("core", "x", "y"), IN_CHIPS)
 
     cosv = jnp.cos(phase)
     sinv = jnp.sin(phase)
@@ -274,7 +285,7 @@
         scalars=1,
         scratch=[pltpu.VMEM((2 * GR * 16, 128), F32)],
     )
-    y2 = a2a(picked.reshape(NZ, 8, CW), "z").reshape(NZ * 8, CW)
+    y2 = a2a(picked.reshape(NZ, 8, CW), "z", ALONG_Z).reshape(NZ * 8, CW)
 
     (spread,) = call(
         spread_kernel,
@@ -285,7 +296,7 @@
         away=(0,),
         scratch=[pltpu.VMEM((SLOTS, CW), BF), pltpu.SemaphoreType.DMA((NG,))],
     )
-    rows = a2a(spread, ("x", "y"))
+    rows = a2a(spread, ("x", "y"), IN_PLANE)
     (info,) = call(
         info_kernel,
         "info",
@@ -305,11 +316,11 @@
         far=(0,),
         scratch=[pltpu.VMEM((NG, COMB, CW), BF), pltpu.SemaphoreType.DMA((NG,))],
     )
-    l4 = a2a(lse, ("core", "x", "y"))
+    l4 = a2a(lse, ("core", "x", "y"), IN_CHIPS)
     (merged,) = call(
         merge_kernel, "merge", [l4], [pltpu.VMEM((NZ, NC, 128), F32)], near=(0,)
     )
-    l5 = a2a(merged, "z")
+    l5 = a2a(merged, "z", ALONG_Z)
 
     back, ev = call(
         back_kernel,

time: 144 us -> 133 us (0.924)
  blocking collectives: 71.9 us -> 53.3 us
  starting transfers between devices: 14.2 us -> 21.6 us
    all_to_all x3, blocking collectives: 71.9 us -> 53.3 us  [a2a(): lax.all_to_all(v, axes, split_axis=0, concat_axis=0, tiled=True, axis_ind...]
    all_to_all x2, starting transfers between devices: 14.2 us -> 21.6 us  [a2a(): lax.all_to_all(v, axes, split_axis=0, concat_axis=0, tiled=True, axis_ind...]
where the time goes in v3:
time: 133 us; the launch traced here: 132 us
  blocking collectives  53.3 us (40%)
  waiting for transfers between devices  34 us (26%)
  starting transfers between devices  21.6 us (16%)
  Pallas kernels  16.9 us (13%)
  local copies, waits for them, and re-layouts  5.24 us (4%)
    all_to_all x3, blocking collectives, a2a(): lax.all_to_all(v, axes, split_axis=0, concat_axis=0, tiled=True, axis_ind...  53.3 us
    all_to_all x2, waiting for transfers between devices, a2a(): lax.all_to_all(v, axes, split_axis=0, concat_axis=0, tiled=True, axis_ind...  34 us
    all_to_all x2, starting transfers between devices, a2a(): lax.all_to_all(v, axes, split_axis=0, concat_axis=0, tiled=True, axis_ind...  21.6 us
    pallas_call x8, Pallas kernels, call(): pl.pallas_call(kernel, in_specs=[smem() if n < scalars else anywhere() if...  16.9 us
    unnamed x16, local copies, waits for them, and re-layouts  3.44 us
  transfers between devices with their start and end apart: 2, of which 2 were waited for; matrix products, arithmetic and copies ran while one was open for 1% of the time, Pallas kernels for 3%

profile of v3, /device:TPU:1, one launch (start us, length us, event | category | flops | bytes accessed | tf_op | source)
XLA Modules:
  0.0 131.8 jit_solution(13708969960040791180)
XLA Ops:
  0.6 0.0 copy-start.5
  0.6 0.8 copy-done.5
  1.5 0.0 copy-start.7
  1.5 0.7 copy-done.7
  2.1 1.3 prepare.1
  3.4 13.9 %all-to-all-start = ((bf16[32,16,128]{2,1,0:T(8,128)(2,1)}), bf16[32,16,128]{2,1,0:T(8,128)(2,1)S(1)}, u32[]{:S(2)}, u32[]{:S(2)}) async-start(bf16[32,16,128]{2,1,0:T(8,128)(2,1)} %prepare.1), calls=%async_computation | async-start | bytes 262144 | tf_op jit(solution)/shard_map/all_to_all | solution.py:226
  17.3 0.1 pad_add_fusion.idx_ref
  17.4 2.7 %all-to-all-done.x_ref = bf16[32,16,128]{2,1,0:T(8,128)(2,1)S(1)} async-done(((bf16[32,16,128]{2,1,0:T(8,128)(2,1)}), bf16[32,16,128]{2,1,0:T(8,128)(2,1)S(1)}, u32[]{:S(2)}, u32[]{:S(2)}) %all-to-all-start) | async-done | bytes 131104 | tf_op jit(solution)/shard_map/all_to_all | solution.py:226
  20.1 1.4 %select.7 = (bf16[128,1024]{1,0:T(8,128)(2,1)S(1)}, f32[8,128]{1,0:T(8,128)}) custom-call(s32[3]{0:T(128)S(1)} %pad_add_fusion.idx_ref, bf16[32,16,128]{2,1,0:T(8,128)(2,1)S(1)} %all-to-all-done.x_ref), custom_call_target="tpu_custom_call" | custom-call | tf_op jit(solution)/shard_map/select/pallas_call | solution.py:238
  21.4 27.2 %all_to_all.25 = bf16[16,8,1024]{2,1,0:T(8,128)(2,1)S(1)} all-to-all(bf16[16,8,1024]{2,1,0:T(8,128)(2,1)S(1)} %bitcast.11), channel_id=1, replica_groups={{16,18,20,22,24,26,28,30,0,2,4,6,8,10,12,14},{17,19,21,23,25,27,29,31,1..., dimensions={0} | all-to-all | bytes 524288 | tf_op jit(solution)/shard_map/all_to_all | solution.py:226
  48.7 2.0 %spread.1 = bf16[16,96,1024]{2,1,0:T(8,128)(2,1)} custom-call(bf16[128,1024]{1,0:T(8,128)(2,1)S(1)} %bitcast.8), custom_call_target="tpu_custom_call" | custom-call | tf_op jit(solution)/shard_map/spread/pallas_call | solution.py:238
  50.7 7.7 %all-to-all-start.2 = ((bf16[16,96,1024]{2,1,0:T(8,128)(2,1)}), bf16[16,96,1024]{2,1,0:T(8,128)(2,1)S(1)}, u32[]{:S(2)}, u32[]{:S(2)}) async-start(bf16[16,96,1024]{2,1,0:T(8,128)(2,1)} %spread.1), calls=%async_computation.2 | async-start | bytes 6291456 | tf_op jit(solution)/shard_map/all_to_all | solution.py:226
  58.4 0.0 copy-start.6
  58.4 1.8 %fusion = (f32[4,8192]{1,0:T(4,128)S(1)}, f32[4,8192]{1,0:T(4,128)S(1)}) fusion(f32[4,8192]{1,0:T(4,128)} %param.7), kind=kLoop, calls=%fused_computation.1 | loop fusion | bytes 393216 | tf_op jit(solution)/shard_map/sin | solution.py:271
  60.2 0.0 copy-start.1
  60.2 0.0 copy-start
  60.2 0.0 copy-start.2
  60.2 1.3 copy-done.2
  61.5 3.0 %rotate.1.t_ref = bf16[16,128,1024]{2,1,0:T(8,128)(2,1)} custom-call(bf16[32,16384]{1,0:T(8,128)(2,1)S(1)} %bitcast.10, f32[4,8192]{1,0:T(4,128)S(1)} %get-tuple-element.19.c_ref.cos_ref, f32[4,8192]{1,0:T(4,128)S(1)} %get-tuple-element.18.s_ref.sin_ref), custom_call_target="tpu_custom_call" | custom-call | tf_op jit(solution)/shard_map/rotate/pallas_call | solution.py:238
  64.5 0.0 copy-done.1
  64.5 0.0 copy-done.6
  64.5 1.0 info.1.info_ref
  65.6 0.0 copy-start.3
  65.6 0.6 copy-done.3
  66.2 31.3 %all-to-all-done.2.r_ref = bf16[16,96,1024]{2,1,0:T(8,128)(2,1)S(1)} async-done(((bf16[16,96,1024]{2,1,0:T(8,128)(2,1)}), bf16[16,96,1024]{2,1,0:T(8,128)(2,1)S(1)}, u32[]{:S(2)}, u32[]{:S(2)}) %all-to-all-start.2) | async-done | bytes 3145760 | tf_op jit(solution)/shard_map/all_to_all | solution.py:226
  97.5 0.0 copy-start.4
  97.5 4.0 %score.1 = (f32[128,128]{1,0:T(8,128)S(1)}, f32[32,1,128]{2,1,0:T(1,128)S(1)}) custom-call(bf16[16,128,1024]{2,1,0:T(8,128)(2,1)} %rotate.1.t_ref, bf16[16,96,1024]{2,1,0:T(8,128)(2,1)S(1)} %all-to-all-done.2.r_ref), custom_call_target="tpu_custom_call" | custom-call | tf_op jit(solution)/shard_map/score/pallas_call | solution.py:238
  101.5 0.0 copy-done
  101.6 12.7 %all_to_all.26.l_ref = f32[32,1,128]{2,1,0:T(1,128)S(1)} all-to-all(f32[32,1,128]{2,1,0:T(1,128)S(1)} %get-tuple-element.13), channel_id=1, replica_groups={{320,352,256,288,448,480,384,416,64,96,0,32,192,224,128,160,321,353,257..., dimensions={0} | all-to-all | bytes 32768 | tf_op jit(solution)/shard_map/all_to_all | solution.py:226
  114.3 13.3 %all_to_all.27.l_ref = f32[16,2,128]{2,1,0:T(2,128)S(1)} all-to-all(f32[16,2,128]{2,1,0:T(2,128)S(1)} %merge.1), channel_id=1, replica_groups={{16,18,20,22,24,26,28,30,0,2,4,6,8,10,12,14},{17,19,21,23,25,27,29,31,1..., dimensions={0} | all-to-all | bytes 32768 | tf_op jit(solution)/shard_map/all_to_all | solution.py:226
  127.7 0.0 copy-done.4
  127.7 4.2 %back.1 = (bf16[32,16384]{1,0:T(8,128)(2,1)}, f32[1,1]{1,0:T(1,128)}) custom-call(f32[16,2,128]{2,1,0:T(2,128)S(1)} %all_to_all.27.l_ref, f32[6,16,128]{2,1,0:T(8,128)S(1)} %copy-done.4, f32[128,128]{1,0:T(8,128)S(1)} %get-tuple-element.15.score_ref, bf16[16,96,1024]{2,1,0:T(8,128)(2,1)S(1)} %all-to-all-done.2.r_ref, f32[4,8192]{1,0:T(4,128)} %copy-done.1, ...), custom_call_target="tpu_custom_call" | custom-call | tf_op jit(solution)/shard_map/back/pallas_call | solution.py:238
  (1 shorter events, 0.0 us)
Async XLA Ops:
  0.6 0.8 copy-start.5
  1.5 0.7 copy-start.7
  3.4 16.7 %all-to-all-start = ((bf16[32,16,128]{2,1,0:T(8,128)(2,1)}), bf16[32,16,128]{2,1,0:T(8,128)(2,1)S(1)}, u32[]{:S(2)}, u32[]{:S(2)}) async-start(bf16[32,16,128]{2,1,0:T(8,128)(2,1)} %prepare.1), calls=%async_computation | async-start | bytes 262144 | tf_op jit(solution)/shard_map/all_to_all | solution.py:226
  50.7 46.8 %all-to-all-start.2 = ((bf16[16,96,1024]{2,1,0:T(8,128)(2,1)}), bf16[16,96,1024]{2,1,0:T(8,128)(2,1)S(1)}, u32[]{:S(2)}, u32[]{:S(2)}) async-start(bf16[16,96,1024]{2,1,0:T(8,128)(2,1)} %spread.1), calls=%async_computation.2 | async-start | bytes 6291456 | tf_op jit(solution)/shard_map/all_to_all | solution.py:226
  58.4 6.1 %copy-start.6 = (f32[8,128]{1,0:T(8,128)S(1)}, f32[8,128]{1,0:T(8,128)}, u32[]{:S(2)}) copy-start(f32[8,128]{1,0:T(8,128)} %get-tuple-element.11.own_ref) | copy-start | bytes 12292
  60.2 4.3 %copy-start.1 = (f32[4,8192]{1,0:T(4,128)}, f32[4,8192]{1,0:T(4,128)S(1)}, u32[]{:S(2)}) copy-start(f32[4,8192]{1,0:T(4,128)S(1)} %get-tuple-element.19.c_ref.cos_ref) | copy-start | bytes 393220
  60.2 41.3 %copy-start = (f32[4,8192]{1,0:T(4,128)}, f32[4,8192]{1,0:T(4,128)S(1)}, u32[]{:S(2)}) copy-start(f32[4,8192]{1,0:T(4,128)S(1)} %get-tuple-element.18.s_ref.sin_ref) | copy-start | bytes 393220
  60.2 1.3 %copy-start.2 = (bf16[2,16,16384]{2,1,0:T(8,128)(2,1)S(1)}, bf16[2,16,16384]{2,1,0:T(8,128)(2,1)}, u32[]{:S(2)}) copy-start(bf16[2,16,16384]{2,1,0:T(8,128)(2,1)} %param.6) | copy-start | bytes 3145732
  65.6 0.6 copy-start.3
  97.5 30.2 %copy-start.4 = (f32[6,16,128]{2,1,0:T(8,128)S(1)}, f32[6,16,128]{2,1,0:T(8,128)}, u32[]{:S(2)}) copy-start(f32[6,16,128]{2,1,0:T(8,128)} %copy-done.3) | copy-start | bytes 147460

commit v4 on v3

--- a/solution.py
+++ b/solution.py
@@ -24,10 +24,21 @@
 SLOTS = 2 * GR * CAP
 
 FIRST_Z = 8
-PLANE = [((i // NY + 2) % NX) * NY + (i % NY + 2) % NY for i in range(NG)]
+TURN = [2, 3, 0, 1]
+PLANES = [
+    [x * NY + y for y in TURN for x in TURN],
+    [x * NY + y for x in TURN for y in TURN],
+]
 ALONG_Z = [[(i + FIRST_Z) % NZ for i in range(NZ)]]
-IN_PLANE = [PLANE]
-IN_CHIPS = [PLANE + [NG + g for g in PLANE]]
+IN_CHIPS = [PLANES[0] + [NG + g for g in PLANES[1]]]
+LINES = (
+    [[x * NY + y for x in TURN] for y in range(NY)],
+    [[x * NY + y for y in TURN] for x in range(NX)],
+)
+STAGES = [
+    LINES[c] + [[NG + g for g in line] for line in LINES[1 - c]] for c in range(2)
+]
+AHEAD = 16
 
 
 def iota(shape, dim):
@@ -54,11 +65,19 @@
     return pl.BlockSpec(memory_space=pltpu.SMEM)
 
 
-def prepare_kernel(sig_ref, x_ref, out_ref, scr):
+def prepare_kernel(sig_hbm, x_hbm, out_ref, sig_ref, x_ref, scr, sem):
+    copies = [
+        pltpu.make_async_copy(sig_hbm, sig_ref, sem.at[0]),
+        pltpu.make_async_copy(x_hbm, x_ref, sem.at[1]),
+    ]
+    for c in copies:
+        c.start()
+    scr[...] = jnp.zeros((NG * 16, 128), F32)
+    for c in copies:
+        c.wait()
     lane = iota((1, 128), 1)
     hit = (lane == sig_ref[0, 0]) | (lane == sig_ref[0, 1]) | (lane == sig_ref[0, 2])
     member = jnp.where(hit, 1.0, 0.0)
-    scr[...] = jnp.zeros((NG * 16, 128), F32)
     scr[pl.ds(8, NG, stride=16), :] = jnp.broadcast_to(member, (NG, 128))
     x = x_ref[...].astype(F32)
     for g in range(NG):
@@ -107,7 +126,15 @@
     s = iota((SLOTS, 128), 0)
     compact = jnp.where(iota((SLOTS, 128), 1) == (s // 6) * 8 + s % 6, 1.0, 0.0).astype(BF)
     scr[...] = nn_dot(compact, y_ref[...]).astype(BF)
-    copies = [pltpu.make_async_copy(scr, out_ref.at[g], sem.at[g]) for g in range(NG)]
+    copies = [pltpu.make_async_copy(scr, out_ref.at[g], sem.at[g]) for g in range(NX)]
+    for c in copies:
+        c.start()
+    for c in copies:
+        c.wait()
+
+
+def repeat_kernel(y_ref, out_ref, sem):
+    copies = [pltpu.make_async_copy(y_ref, out_ref.at[g], sem.at[g]) for g in range(NX)]
     for c in copies:
         c.start()
     for c in copies:
@@ -150,11 +177,13 @@
 
 def score_kernel(t_ref, r_ref, score_ref, lse_ref, scr, sem):
     copies = [pltpu.make_async_copy(t_ref.at[g], scr.at[g], sem.at[g]) for g in range(NG)]
-    for c in copies:
-        c.start()
+    for g in range(AHEAD):
+        copies[g].start()
     acc = jnp.zeros((COMB, SLOTS), F32)
     for g in range(NG):
         copies[g].wait()
+        if g + AHEAD < NG:
+            copies[g + AHEAD].start()
         acc = acc + nt_dot(scr[g], r_ref[g])
     score_ref[...] = jnp.zeros((COMB, 128), F32)
     score_ref[:, :SLOTS] = acc
@@ -253,17 +282,22 @@
     core = lax.axis_index("core")
     z = lax.axis_index("z")
     block = 2 * ((z - FIRST_Z) % NZ) + core
-    x, y = lax.axis_index("x"), lax.axis_index("y")
-    place = ((x + 2) % NX) * NY + (y + 2) % NY
+    x, y = (lax.axis_index("x") + 2) % NX, (lax.axis_index("y") + 2) % NY
+    place = jnp.where(core == 0, y * NX + x, x * NY + y)
     idx = jnp.stack([core, block, place]).astype(I32)
 
     (first,) = call(
         prepare_kernel,
         "prepare",
         [significant, images],
-        [pltpu.VMEM((NC * NG, 16, 128), BF)],
-        scalars=1,
-        scratch=[pltpu.VMEM((NG * 16, 128), F32)],
+        [pltpu.HBM((NC * NG, 16, 128), BF)],
+        far=(0, 1),
+        scratch=[
+            pltpu.SMEM((1, 3), I32),
+            pltpu.VMEM((1, 2 * COEF), BF),
+            pltpu.VMEM((NG * 16, 128), F32),
+            pltpu.SemaphoreType.DMA((2,)),
+        ],
     )
     x1 = a2a(first, ("core", "x", "y"), IN_CHIPS)
 
@@ -291,12 +325,22 @@
         spread_kernel,
         "spread",
         [y2],
-        [pltpu.HBM((NG, SLOTS, CW), BF)],
+        [pltpu.HBM((NX, SLOTS, CW), BF)],
         near=(0,),
         away=(0,),
-        scratch=[pltpu.VMEM((SLOTS, CW), BF), pltpu.SemaphoreType.DMA((NG,))],
-    )
-    rows = a2a(spread, ("x", "y"), IN_PLANE)
+        scratch=[pltpu.VMEM((SLOTS, CW), BF), pltpu.SemaphoreType.DMA((NX,))],
+    )
+    line = a2a(spread, ("core", "x", "y"), STAGES[0])
+    (lines,) = call(
+        repeat_kernel,
+        "repeat",
+        [line],
+        [pltpu.HBM((NX, NX, SLOTS, CW), BF)],
+        near=(0,),
+        away=(0,),
+        scratch=[pltpu.SemaphoreType.DMA((NX,))],
+    )
+    rows = a2a(lines, ("core", "x", "y"), STAGES[1]).reshape(NG, SLOTS, CW)
     (info,) = call(
         info_kernel,
         "info",

time: 133 us -> 121 us (0.910)
  waiting for transfers between devices: 34 us -> 13.9 us
  blocking collectives: 53.3 us -> 65.5 us
  starting transfers between devices: 21.6 us -> 18.4 us
  local copies, waits for them, and re-layouts: 5.24 us -> 3.74 us
    all_to_all x2, waiting for transfers between devices: 34 us -> 13.9 us  [a2a(): lax.all_to_all(v, axes, split_axis=0, concat_axis=0, tiled=True, axis_ind...]
    all_to_all x3 -> x4, blocking collectives: 53.3 us -> 65.5 us  [a2a(): lax.all_to_all(v, axes, split_axis=0, concat_axis=0, tiled=True, axis_ind...]
    all_to_all x2, starting transfers between devices: 21.6 us -> 18.4 us  [a2a(): lax.all_to_all(v, axes, split_axis=0, concat_axis=0, tiled=True, axis_ind...]
    unnamed x16 -> x12, local copies, waits for them, and re-layouts: 3.44 us -> 1.96 us
    pallas_call x8 -> x9, Pallas kernels: 16.9 us -> 18 us  [call(): pl.pallas_call(kernel, in_specs=[smem() if n < scalars else anywhere() if...]
  transfers between devices with their start and end apart: 2 -> 2, of which waited for: 2 -> 2; matrix products, arithmetic and copies ran while one was open for 1% -> 2% of each run, Pallas kernels for 3% -> 3%
where the time goes in v4:
time: 121 us; the launch traced here: 120 us
  blocking collectives  65.5 us (54%)
  starting transfers between devices  18.4 us (15%)
  Pallas kernels  18 us (15%)
  waiting for transfers between devices  13.9 us (11%)
  local copies, waits for them, and re-layouts  3.74 us (3%)
    all_to_all x4, blocking collectives, a2a(): lax.all_to_all(v, axes, split_axis=0, concat_axis=0, tiled=True, axis_ind...  65.5 us
    all_to_all x2, starting transfers between devices, a2a(): lax.all_to_all(v, axes, split_axis=0, concat_axis=0, tiled=True, axis_ind...  18.4 us
    pallas_call x9, Pallas kernels, call(): pl.pallas_call(kernel, in_specs=[smem() if n < scalars else anywhere() if...  18 us
    all_to_all x2, waiting for transfers between devices, a2a(): lax.all_to_all(v, axes, split_axis=0, concat_axis=0, tiled=True, axis_ind...  13.9 us
  transfers between devices with their start and end apart: 2, of which 2 were waited for; matrix products, arithmetic and copies ran while one was open for 2% of the time, Pallas kernels for 3%

profile of v4, /device:TPU:1, one launch (start us, length us, event | category | flops | bytes accessed | tf_op | source)
XLA Modules:
  0.0 120.4 jit_solution(13982465525317484988)
XLA Ops:
  0.6 1.6 %prepare.1 = bf16[32,16,128]{2,1,0:T(8,128)(2,1)} custom-call(s32[1,3]{1,0:T(1,128)} %sig_hbm.1, bf16[1,16384]{1,0:T(2,128)(2,1)} %x_hbm.1), custom_call_target="tpu_custom_call" | custom-call | tf_op jit(solution)/shard_map/prepare/pallas_call | solution.py:267
  2.2 13.9 %all-to-all-start = ((bf16[32,16,128]{2,1,0:T(8,128)(2,1)}), bf16[32,16,128]{2,1,0:T(8,128)(2,1)S(1)}, u32[]{:S(2)}, u32[]{:S(2)}) async-start(bf16[32,16,128]{2,1,0:T(8,128)(2,1)} %prepare.1), calls=%async_computation | async-start | bytes 262144 | tf_op jit(solution)/shard_map/all_to_all | solution.py:255
  16.1 0.1 pad_add_fusion.idx_ref
  16.2 2.8 %all-to-all-done.x_ref = bf16[32,16,128]{2,1,0:T(8,128)(2,1)S(1)} async-done(((bf16[32,16,128]{2,1,0:T(8,128)(2,1)}), bf16[32,16,128]{2,1,0:T(8,128)(2,1)S(1)}, u32[]{:S(2)}, u32[]{:S(2)}) %all-to-all-start) | async-done | bytes 131104 | tf_op jit(solution)/shard_map/all_to_all | solution.py:255
  19.0 1.3 %select.7 = (bf16[128,1024]{1,0:T(8,128)(2,1)S(1)}, f32[8,128]{1,0:T(8,128)}) custom-call(s32[3]{0:T(128)S(1)} %pad_add_fusion.idx_ref, bf16[32,16,128]{2,1,0:T(8,128)(2,1)S(1)} %all-to-all-done.x_ref), custom_call_target="tpu_custom_call" | custom-call | tf_op jit(solution)/shard_map/select/pallas_call | solution.py:267
  20.3 27.3 %all_to_all.30 = bf16[16,8,1024]{2,1,0:T(8,128)(2,1)S(1)} all-to-all(bf16[16,8,1024]{2,1,0:T(8,128)(2,1)S(1)} %bitcast.14), channel_id=1, replica_groups={{16,18,20,22,24,26,28,30,0,2,4,6,8,10,12,14},{17,19,21,23,25,27,29,31,1..., dimensions={0} | all-to-all | bytes 524288 | tf_op jit(solution)/shard_map/all_to_all | solution.py:255
  47.7 1.1 spread.1
  48.8 12.2 %all_to_all.31.y_ref = bf16[4,96,1024]{2,1,0:T(8,128)(2,1)S(1)} all-to-all(bf16[4,96,1024]{2,1,0:T(8,128)(2,1)} %spread.1), channel_id=1, replica_groups={{256,384,0,128},{288,416,32,160},{320,448,64,192},{352,480,96,224},{65,..., dimensions={0} | all-to-all | bytes 1572864 | tf_op jit(solution)/shard_map/all_to_all | solution.py:255
  60.9 1.7 %repeat.1 = bf16[4,4,96,1024]{3,2,1,0:T(8,128)(2,1)} custom-call(bf16[4,96,1024]{2,1,0:T(8,128)(2,1)S(1)} %all_to_all.31.y_ref), custom_call_target="tpu_custom_call" | custom-call | tf_op jit(solution)/shard_map/repeat/pallas_call | solution.py:267
  62.7 4.5 %all-to-all-start.3 = ((bf16[4,4,96,1024]{3,2,1,0:T(8,128)(2,1)}), bf16[4,4,96,1024]{3,2,1,0:T(8,128)(2,1)S(1)}, u32[]{:S(2)}, u32[]{:S(2)}) async-start(bf16[4,4,96,1024]{3,2,1,0:T(8,128)(2,1)} %repeat.1), calls=%async_computation.3 | async-start | bytes 6291456 | tf_op jit(solution)/shard_map/all_to_all | solution.py:255
  67.2 0.0 copy-start.5
  67.2 1.8 %fusion = (f32[4,8192]{1,0:T(4,128)S(1)}, f32[4,8192]{1,0:T(4,128)S(1)}) fusion(f32[4,8192]{1,0:T(4,128)} %param.7), kind=kLoop, calls=%fused_computation.1 | loop fusion | bytes 393216 | tf_op jit(solution)/shard_map/sin | solution.py:305
  69.0 0.0 copy-start.1
  69.0 0.0 copy-start
  69.0 0.0 copy-start.2
  69.0 1.3 %copy-done.2 = bf16[2,16,16384]{2,1,0:T(8,128)(2,1)S(1)} copy-done((bf16[2,16,16384]{2,1,0:T(8,128)(2,1)S(1)}, bf16[2,16,16384]{2,1,0:T(8,128)(2,1)}, u32[]{:S(2)}) %copy-start.2) | copy-done | bytes 1048600
  70.3 3.0 %rotate.1.t_ref = bf16[16,128,1024]{2,1,0:T(8,128)(2,1)} custom-call(bf16[32,16384]{1,0:T(8,128)(2,1)S(1)} %bitcast.13, f32[4,8192]{1,0:T(4,128)S(1)} %get-tuple-element.19.c_ref.cos_ref, f32[4,8192]{1,0:T(4,128)S(1)} %get-tuple-element.18.s_ref.sin_ref), custom_call_target="tpu_custom_call" | custom-call | tf_op jit(solution)/shard_map/rotate/pallas_call | solution.py:267
  73.3 0.0 copy-done.1
  73.3 0.0 copy-done.5
  73.3 1.0 info.1.info_ref
  74.4 0.0 copy-start.3
  74.4 0.6 copy-done.3
  75.0 11.1 %all-to-all-done.3 = bf16[4,4,96,1024]{3,2,1,0:T(8,128)(2,1)S(1)} async-done(((bf16[4,4,96,1024]{3,2,1,0:T(8,128)(2,1)}), bf16[4,4,96,1024]{3,2,1,0:T(8,128)(2,1)S(1)}, u32[]{:S(2)}, u32[]{:S(2)}) %all-to-all-start.3) | async-done | bytes 3145760 | tf_op jit(solution)/shard_map/all_to_all | solution.py:255
  86.1 0.0 copy-start.4
  86.1 4.0 %score.1 = (f32[128,128]{1,0:T(8,128)S(1)}, f32[32,1,128]{2,1,0:T(1,128)S(1)}) custom-call(bf16[16,128,1024]{2,1,0:T(8,128)(2,1)} %rotate.1.t_ref, bf16[16,96,1024]{2,1,0:T(8,128)(2,1)S(1)} %bitcast.9), custom_call_target="tpu_custom_call" | custom-call | tf_op jit(solution)/shard_map/score/pallas_call | solution.py:267
  90.1 0.0 copy-done
  90.1 12.6 %all_to_all.32.l_ref = f32[32,1,128]{2,1,0:T(1,128)S(1)} all-to-all(f32[32,1,128]{2,1,0:T(1,128)S(1)} %get-tuple-element.13), channel_id=1, replica_groups={{320,448,64,192,352,480,96,224,256,384,0,128,288,416,32,160,321,353,257..., dimensions={0} | all-to-all | bytes 32768 | tf_op jit(solution)/shard_map/all_to_all | solution.py:255
  102.8 13.3 %all_to_all.33.l_ref = f32[16,2,128]{2,1,0:T(2,128)S(1)} all-to-all(f32[16,2,128]{2,1,0:T(2,128)S(1)} %merge.1), channel_id=1, replica_groups={{16,18,20,22,24,26,28,30,0,2,4,6,8,10,12,14},{17,19,21,23,25,27,29,31,1..., dimensions={0} | all-to-all | bytes 32768 | tf_op jit(solution)/shard_map/all_to_all | solution.py:255
  116.2 0.0 copy-done.4
  116.2 4.2 %back.1 = (bf16[32,16384]{1,0:T(8,128)(2,1)}, f32[1,1]{1,0:T(1,128)}) custom-call(f32[16,2,128]{2,1,0:T(2,128)S(1)} %all_to_all.33.l_ref, f32[6,16,128]{2,1,0:T(8,128)S(1)} %copy-done.4, f32[128,128]{1,0:T(8,128)S(1)} %get-tuple-element.15.score_ref, bf16[16,96,1024]{2,1,0:T(8,128)(2,1)S(1)} %bitcast.10, f32[4,8192]{1,0:T(4,128)} %copy-done.1, f32[4,8192]{1,0:T(4,128)} %copy-done), custom_call_target="tpu_custom_call" | custom-call | tf_op jit(solution)/shard_map/back/pallas_call | solution.py:267
  (1 shorter events, 0.0 us)
Async XLA Ops:
  2.2 16.8 %all-to-all-start = ((bf16[32,16,128]{2,1,0:T(8,128)(2,1)}), bf16[32,16,128]{2,1,0:T(8,128)(2,1)S(1)}, u32[]{:S(2)}, u32[]{:S(2)}) async-start(bf16[32,16,128]{2,1,0:T(8,128)(2,1)} %prepare.1), calls=%async_computation | async-start | bytes 262144 | tf_op jit(solution)/shard_map/all_to_all | solution.py:255
  62.7 23.4 %all-to-all-start.3 = ((bf16[4,4,96,1024]{3,2,1,0:T(8,128)(2,1)}), bf16[4,4,96,1024]{3,2,1,0:T(8,128)(2,1)S(1)}, u32[]{:S(2)}, u32[]{:S(2)}) async-start(bf16[4,4,96,1024]{3,2,1,0:T(8,128)(2,1)} %repeat.1), calls=%async_computation.3 | async-start | bytes 6291456 | tf_op jit(solution)/shard_map/all_to_all | solution.py:255
  67.2 6.1 %copy-start.5 = (f32[8,128]{1,0:T(8,128)S(1)}, f32[8,128]{1,0:T(8,128)}, u32[]{:S(2)}) copy-start(f32[8,128]{1,0:T(8,128)} %get-tuple-element.11.own_ref) | copy-start | bytes 12292
  69.0 4.3 %copy-start.1 = (f32[4,8192]{1,0:T(4,128)}, f32[4,8192]{1,0:T(4,128)S(1)}, u32[]{:S(2)}) copy-start(f32[4,8192]{1,0:T(4,128)S(1)} %get-tuple-element.19.c_ref.cos_ref) | copy-start | bytes 393220
  69.0 21.1 %copy-start = (f32[4,8192]{1,0:T(4,128)}, f32[4,8192]{1,0:T(4,128)S(1)}, u32[]{:S(2)}) copy-start(f32[4,8192]{1,0:T(4,128)S(1)} %get-tuple-element.18.s_ref.sin_ref) | copy-start | bytes 393220
  69.0 1.3 %copy-start.2 = (bf16[2,16,16384]{2,1,0:T(8,128)(2,1)S(1)}, bf16[2,16,16384]{2,1,0:T(8,128)(2,1)}, u32[]{:S(2)}) copy-start(bf16[2,16,16384]{2,1,0:T(8,128)(2,1)} %param.6) | copy-start | bytes 3145732
  74.4 0.6 copy-start.3
  86.1 30.1 %copy-start.4 = (f32[6,16,128]{2,1,0:T(8,128)S(1)}, f32[6,16,128]{2,1,0:T(8,128)}, u32[]{:S(2)}) copy-start(f32[6,16,128]{2,1,0:T(8,128)} %copy-done.3) | copy-start | bytes 147460
